TPU v7x, 32 devices: a whole 2x2x4 slice. The times are simulated.
32 devices in a mesh: gx: 2 (over x), gy: 4 (over y, core), gz: 4 (over z).
Axes of the slice: x: 2, y: 2, z: 4, core: 2. Of those that a mesh axis runs over, the one named last changes fastest.
Arguments:
- velocity: float32 [3, 32, 64, 512], P(None, 'gx', 'gy', 'gz'), may hold values from -6 to 6
- gradients: bfloat16 [2, 3, 32, 64, 512], P(None, None, 'gx', 'gy', 'gz'), may hold values from -6 to 6
- shift_x: int32 [2, 4, 8, 4], P(None, 'gx', 'gy', 'gz'), may hold values from -6 to 6
- shift_y: int32 [2, 4, 8, 4], P(None, 'gx', 'gy', 'gz'), may hold values from -6 to 6
- shift_z: int32 [2, 4, 8, 4], P(None, 'gx', 'gy', 'gz'), may hold values from -14 to 14
- fractions: int32 [2, 3, 4, 8, 4], P(None, None, 'gx', 'gy', 'gz'), may hold values from 0 to 7
Outputs:
- hess_vec: float32 [3, 32, 64, 512], P(None, 'gx', 'gy', 'gz')
All inputs are finite; a program needn't handle non-finite values.
Results may differ from a plain program's by a relative error of at most 0.0003.
Values sent between devices are 32-bit elements; how exact they have to be, the bound alone decides.
A program may use at most 64 MiB of HBM per device.

v0:
```python
import functools

import jax
import jax.numpy as jnp
from jax import lax
from jax.experimental import pallas as pl
from jax.experimental.pallas import tpu as pltpu
from jax.sharding import PartitionSpec as P

BX = 8
BY = 8
BZ = 128
RX = 6
RY = 6
RZ = 14
STEPS = 2

STEP_SIZE = 0.5
REG_WEIGHT = 0.1
LAPLACE_TAPS = (-205.0 / 72.0, 8.0 / 5.0, -1.0 / 5.0, 8.0 / 315.0, -1.0 / 560.0)

HX = RX + 2
HY = RY + 2
HZ = RZ + 2
LANES = 128
PK = LANES // HZ
XG = HX // PK
LH = 4
VPK = LANES // (2 * LH)
WX = BX + 2 * HX
WY = BY + 2 * HY
MESH = pl.DeviceIdType.MESH
AXES = ("gx", "gy", "gz")
WAYS = sorted(((i, j, k) for i in (-1, 0, 1) for j in (-1, 0, 1) for k in (-1, 0, 1) if (i, j, k) != (0, 0, 0)),
              key=lambda d: -sum(map(abs, d)))


def piece(way, own, halo):
    return {-1: (0, halo), 0: (halo, halo + own), 1: (halo + own, 2 * halo + own)}[way]


def border(way, own, halo):
    return {-1: (halo, 2 * halo), 0: (halo, halo + own), 1: (own, halo + own)}[way]


def kernel(shape, vel_in, grad_in, shx_in, shy_in, shz_in, frac_in, out,
           vel, grad, shx, shy, shz, frac, arrive,
           E0, E1, U, YP, XP, ACC0, ACC1, T, ST, ADJ, SP, SUM,
           VE, YSU, YSD, YVD, YVU, SV, VRD, VRU, *rest):
    back, (send, recv) = rest[:-2], rest[-2:]
    TX, TY, TZ = vel.shape[1:]
    NBX, NBY = TX // BX, TY // BY
    EX = TX + 2 * HX
    EG = EX // PK
    G = TX // PK
    OX = slice(HX, HX + TX)
    OY = slice(HY, HY + TY)

    at = {a: lax.axis_index(a) for a in AXES}

    def has(way):
        ok = None
        for a, w in zip(AXES, way):
            if w:
                one = at[a] < shape[a] - 1 if w > 0 else at[a] > 0
                ok = one if ok is None else jnp.logical_and(ok, one)
        return ok

    def device(way):
        return {a: at[a] + w for a, w in zip(AXES, way) if w}

    loads = [pltpu.make_async_copy(a, b, arrive.at[n]) for n, (a, b) in enumerate((
        (vel_in, vel), (grad_in, grad), (shx_in, shx), (shy_in, shy), (shz_in, shz), (frac_in, frac)))]
    for load in loads:
        load.start()

    sends = []

    class Copy:
        def __init__(self, src, dst, way):
            i = len(sends)
            self.desc = pltpu.make_async_remote_copy(
                src_ref=src, dst_ref=dst, send_sem=send.at[i], recv_sem=recv.at[i],
                device_id=device(way), device_id_type=MESH)
            self.out, self.into = has(way), has(tuple(-w for w in way))
            sends.append(self)

        def start(self):
            pl.when(self.out)(self.desc.start)
            return self

        def landed(self):
            pl.when(self.into)(self.desc.wait_recv)

        def left(self):
            pl.when(self.out)(self.desc.wait_send)

    lane = lax.broadcasted_iota(jnp.int32, (1, 1, LANES), 2)
    lane2 = lax.broadcasted_iota(jnp.int32, (1, LANES), 1)

    for ref in (E0, E1, VE, YVD, YVU, VRD, VRU) + tuple(back):
        ref[...] = jnp.zeros_like(ref)

    barrier = pltpu.get_barrier_semaphore()
    total = jnp.int32(0)
    for way in WAYS:
        @pl.when(has(way))
        def _(way=way):
            pl.semaphore_signal(barrier, inc=1, device_id=device(way), device_id_type=MESH)
        total = total + has(way).astype(jnp.int32)

    group = lane2 // HZ

    def packed(layer, g):
        first = last = None
        for j in range(PK):
            turned = pltpu.roll(layer(PK * g + j), HZ * j, 1) if j else layer(PK * g)
            first = turned if j == 0 else jnp.where(group == j, turned, first)
            last = turned if j == 0 else jnp.where(group == j - 1, turned, last)
        return first, last

    def unpacked(first, last, j):
        both = jnp.where(group == j, first, last)
        return pltpu.roll(both, LANES - HZ * j, 1) if j else both

    def pack_own(E, k):
        def layer(x):
            return E[HX + x, OY, :]
        for g in range(G):
            SP[k, 0, XG + g, OY, :], SP[k, 1, XG + g, OY, :] = packed(layer, g)

    def region(way, dim_of):
        (x0, x1) = dim_of(way[0], G if way[2] else TX, XG if way[2] else HX)
        (y0, y1) = dim_of(way[1], TY, HY)
        return slice(x0, x1), slice(y0, y1)

    def rim(ref, way, where):
        xs, ys = where
        base = {0: 0, -1: EX, 1: EX + EG}[way]
        return ref.at[slice(base + xs.start, base + xs.stop), ys, :]

    def forward_exchange(E, k, between):
        copies = []
        for way in WAYS:
            xs, ys = region(way, border)
            if way[2]:
                src = SP.at[k, 0 if way[2] < 0 else 1, xs, ys, :]
            else:
                src = E.at[xs, ys, :]
            other = tuple(-w for w in way)
            copies.append(Copy(src, rim(E, other[2], region(other, piece)), way).start())
        between()
        for copy in copies:
            copy.landed()

    def unpack(E):
        for g in range(EG):
            below, above = E[EX + g], E[EX + EG + g]
            for j in range(PK):
                U[PK * g + j] = unpacked(above, below, j)

    def taps(k, d, bx, by):
        e = frac[k, bx, by, 0, d].astype(jnp.float32) * 0.125
        e2 = e * e
        e3 = e2 * e
        return (0.5 * (2.0 * e2 - e3 - e), 0.5 * (3.0 * e3 - 5.0 * e2 + 2.0),
                0.5 * (4.0 * e2 - 3.0 * e3 + e), 0.5 * (e3 - e2))

    def gather_block(E, k, bx, by):
        n = bx * NBY + by
        a, b, c = shx[k, bx, 0, by], shy[k, bx, 0, by], shz[k, bx, 0, by]
        wx, wy, wz = (taps(k, d, bx, by) for d in range(3))
        y0 = by * BY
        x0 = bx * BX + (a + HX - 1)
        for i, ref in enumerate((E, U)):
            win = ref[pl.ds(x0, BX + 3), pl.ds(y0, WY), :]
            T[n, i * BX:(i + 1) * BX] = sum(wx[u] * win[u:u + BX] for u in range(4))
        y = sum(wy[v] * T[n, :, pl.ds(b + (HY - 1 + v), BY), :] for v in range(4))
        own, rim = y[:BX].reshape(BX * BY, LANES), y[BX:].reshape(BX * BY, LANES)
        res = None
        for w in range(4):
            s = c + (w - 1)
            inside = jnp.logical_and(lane2 >= s, lane2 < LANES + s)
            term = wz[w] * pltpu.roll(jnp.where(inside, own, rim), lax.rem(LANES - s, LANES), 1)
            res = term if res is None else res + term
        return res.reshape(BX, BY, LANES)

    def spread_block(vals, k, bx, by):
        n = bx * NBY + by
        a, b, c = shx[k, bx, 0, by], shy[k, bx, 0, by], shz[k, bx, 0, by]
        wx, wy, wz = (taps(k, d, bx, by) for d in range(3))
        flat = vals.reshape(BX * BY, LANES)
        own = rim = None
        for w in range(4):
            s = c + (w - 1)
            inside = jnp.logical_and(lane2 >= s, lane2 < LANES + s)
            term = wz[w] * pltpu.roll(flat, lax.rem(LANES + s, LANES), 1)
            o, r = jnp.where(inside, term, 0.0), jnp.where(inside, 0.0, term)
            own, rim = (o, r) if own is None else (own + o, rim + r)
        YP[n, 0:BX, 2 * HY:2 * HY + BY, :] = own.reshape(BX, BY, LANES)
        YP[n, BX:2 * BX, 2 * HY:2 * HY + BY, :] = rim.reshape(BX, BY, LANES)
        t = sum(wy[v] * YP[n, :, pl.ds((HY + 1 - v) - b, WY), :] for v in range(4))
        for i in range(2):
            for m in range(BX + 3):
                XP[n, i, 2 * HX + m] = sum(wx[u] * t[i * BX + m - u] for u in range(4) if 0 <= m - u < BX)

    def collect(ACC, k):
        starts = {(bx, by): (HX + 1) - shx[k, bx, 0, by] for bx in range(NBX) for by in range(NBY)}

        def layer(i, x):
            tiles = [None] * ((TY + 2 * HY) // BY)
            for bx in range(NBX):
                if not 0 <= x - bx * BX < WX:
                    continue
                for by in range(NBY):
                    rows = XP[bx * NBY + by, i, starts[bx, by] + (x - bx * BX)]
                    for q in range(WY // BY):
                        part = rows[q * BY:(q + 1) * BY]
                        old = tiles[by + q]
                        tiles[by + q] = part if old is None else old + part
            return jnp.concatenate(tiles, axis=0)

        for g in range(EG):
            above, below = packed(functools.partial(layer, 1), g)
            ACC[EX + EG + g] = above
            ACC[EX + g] = below
        for x in range(EX):
            ACC[x] = layer(0, x)

    def return_exchange(ACC, k, between):
        copies = []
        for n, way in enumerate(WAYS):
            copies.append((way, back[n].at[k], Copy(
                rim(ACC, way[2], region(way, piece)), back[n].at[k], way).start()))
        between()
        SUM[...] = jnp.zeros_like(SUM)
        for way, came, copy in copies:
            copy.landed()
            other = tuple(-w for w in way)
            xs, ys = region(other, border)
            if way[2]:
                side = 0 if way[2] > 0 else 1
                SUM[side, xs, ys, :] = SUM[side, xs, ys, :] + came[...]
            else:
                ACC[xs, ys, :] = ACC[xs, ys, :] + came[...]
        for g in range(G):
            first, last = SUM[0, XG + g, OY, :], SUM[1, XG + g, OY, :]
            for j in range(PK):
                x = PK * g + j
                edge = jnp.logical_or(lane2 < HZ, lane2 >= LANES - HZ)
                ADJ[x] = ACC[HX + x, OY, :] + jnp.where(edge, unpacked(first, last, j), 0.0)

    def each_block(fn):
        for bx in range(NBX):
            for by in range(NBY):
                fn(bx, by)

    for load in loads:
        load.wait()
    E0[OX, OY, :] = STEP_SIZE * sum(grad[0, c].astype(jnp.float32) * vel[c] for c in range(3))
    pack_own(E0, 0)
    pl.semaphore_wait(barrier, total)

    def prepare():
        for ref in (YP, XP):
            ref[...] = jnp.zeros_like(ref)
        send_faces()

    def nothing():
        pass

    faces = []

    def send_faces():
        VE[:, LH:LH + TX, OY, :] = vel[...]
        for c in range(3):
            for i in range(TX // 2):
                for h in range(2):
                    YSU[c, i, LH * h:LH * (h + 1), :] = vel[c, 2 * i + h, TY - LH:TY, :]
                    YSD[c, i, LH * h:LH * (h + 1), :] = vel[c, 2 * i + h, 0:LH, :]
            for g in range(TX // VPK):
                row = None
                for j in range(VPK):
                    turned = pltpu.roll(vel[c, VPK * g + j], (2 * LH * j + LH) % LANES, 1)
                    row = turned if row is None else jnp.where(lane2 // (2 * LH) == j, turned, row)
                SV[c, g] = row
        faces.extend([
            Copy(SV, VRD, (0, 0, 1)).start(), Copy(SV, VRU, (0, 0, -1)).start(),
            Copy(vel.at[:, TX - LH:TX], VE.at[:, 0:LH, OY, :], (1, 0, 0)).start(),
            Copy(vel.at[:, 0:LH], VE.at[:, LH + TX:2 * LH + TX, OY, :], (-1, 0, 0)).start(),
            Copy(YSU, YVD, (0, 1, 0)).start(), Copy(YSD, YVU, (0, -1, 0)).start()])

    forward_exchange(E0, 0, prepare)
    unpack(E0)

    def first(bx, by):
        y0 = by * BY
        ST[pl.ds(bx * BX, BX), pl.ds(y0, BY), :] = gather_block(E0, 0, bx, by)

    each_block(first)
    g1 = sum(grad[1, c].astype(jnp.float32) * vel[c] for c in range(3))
    E1[OX, OY, :] = ST[...] + STEP_SIZE * g1
    pack_own(E1, 1)

    forward_exchange(E1, 1, nothing)
    unpack(E1)

    def second(bx, by):
        spread_block(gather_block(E1, 1, bx, by), 1, bx, by)

    each_block(second)
    collect(ACC1, 1)

    def regular():
        for f in faces:
            f.landed()
        for c in range(3):
            for i in range(TX // 2):
                for h in range(2):
                    VE[c, LH + 2 * i + h, HY - LH:HY, :] = YVD[c, i, LH * h:LH * (h + 1), :]
                    VE[c, LH + 2 * i + h, HY + TY:HY + TY + LH, :] = YVU[c, i, LH * h:LH * (h + 1), :]
        rows = lax.broadcasted_iota(jnp.int32, (2 * LANES, LANES), 0)
        cols = lax.broadcasted_iota(jnp.int32, (2 * LANES, LANES), 1)
        r = rows - LANES
        place = jnp.where(rows < LANES, rows, jnp.where(r < LH, r + LANES, r - LANES))
        known = jnp.logical_or(rows < LANES, jnp.logical_or(r < LH, r >= LANES - LH))
        gap = jnp.abs(place - cols)
        band = jnp.zeros((2 * LANES, LANES), jnp.float32)
        for k in range(5):
            tap = (3.0 if k == 0 else 1.0) * LAPLACE_TAPS[k]
            band = jnp.where(jnp.logical_and(known, gap == k), tap, band)
        for c in range(3):
            rims = []
            for g in range(TX // VPK):
                row = jnp.where(lane2 % (2 * LH) < LH, VRD[c, g], VRU[c, g])
                for j in range(VPK):
                    rims.append(pltpu.roll(row, (LANES - (2 * LH * j + LH)) % LANES, 1))
            rim = jnp.concatenate(rims, axis=0)
            own = vel[c].reshape(TX * TY, LANES)
            res = jnp.dot(jnp.concatenate([own, rim], axis=1), band,
                          preferred_element_type=jnp.float32,
                          precision=lax.Precision.HIGHEST).reshape(TX, TY, LANES)
            for k in range(1, 5):
                res = res + LAPLACE_TAPS[k] * (
                    VE[c, LH + k:LH + k + TX, OY, :] + VE[c, LH - k:LH - k + TX, OY, :]
                    + VE[c, LH:LH + TX, HY + k:HY + k + TY, :]
                    + VE[c, LH:LH + TX, HY - k:HY - k + TY, :])
            out[c] = (-REG_WEIGHT) * res

    return_exchange(ACC1, 1, regular)

    def third(bx, by):
        y0 = by * BY
        vals = ADJ[pl.ds(bx * BX, BX), pl.ds(y0, BY), :]
        spread_block(vals, 0, bx, by)

    each_block(third)
    collect(ACC0, 0)

    def add_gauss(k):
        for c in range(3):
            out[c] = out[c] + STEP_SIZE * grad[k, c].astype(jnp.float32) * ADJ[...]

    def last():
        add_gauss(1)
        for copy in sends:
            copy.left()

    return_exchange(ACC0, 0, last)
    add_gauss(0)


COPIES = 4 * len(WAYS) + 6


def body(shape, velocity, gradients, shift_x, shift_y, shift_z, fractions):
    TX, TY, TZ = velocity.shape[1:]
    assert TZ == BZ == LANES and TX % VPK == 0 and TX % BX == 0 and TY % BY == 0
    EX, EY = TX + 2 * HX, TY + 2 * HY
    EG, G = EX // PK, TX // PK
    NB = (TX // BX) * (TY // BY)

    def span(way):
        groups = (XG if way[0] else G) if way[2] else (HX if way[0] else TX)
        return groups, HY if way[1] else TY

    vm = lambda *s: pltpu.VMEM(s, jnp.float32)
    vmem = pl.BlockSpec(memory_space=pltpu.VMEM)
    hbm = pl.BlockSpec(memory_space=pltpu.HBM)
    shift_x, shift_y, shift_z = (s.transpose(0, 1, 3, 2) for s in (shift_x, shift_y, shift_z))
    fractions = fractions.transpose(0, 2, 3, 4, 1)
    return pl.pallas_call(
        functools.partial(kernel, shape),
        out_shape=jax.ShapeDtypeStruct(velocity.shape, jnp.float32),
        in_specs=[hbm] * 6,
        out_specs=vmem,
        scratch_shapes=[
            pltpu.VMEM(velocity.shape, velocity.dtype), pltpu.VMEM(gradients.shape, gradients.dtype),
            *[pltpu.SMEM(s.shape, s.dtype) for s in (shift_x, shift_y, shift_z, fractions)],
            pltpu.SemaphoreType.DMA((6,)),
            vm(EX + 2 * EG, EY, LANES), vm(EX + 2 * EG, EY, LANES),
            vm(EX, EY, LANES),
            vm(NB, 2 * BX, 2 * WY - BY, LANES), vm(NB, 2, 2 * WX - BX, WY, LANES),
            vm(EX + 2 * EG, EY, LANES), vm(EX + 2 * EG, EY, LANES),
            vm(NB, 2 * BX, WY, LANES), vm(TX, TY, LANES), vm(TX, TY, LANES),
            vm(2, 2, EG, EY, LANES), vm(2, EG, EY, LANES),
            vm(3, TX + 2 * LH, EY, LANES),
            vm(3, TX // 2, 2 * LH, LANES), vm(3, TX // 2, 2 * LH, LANES),
            vm(3, TX // 2, 2 * LH, LANES), vm(3, TX // 2, 2 * LH, LANES),
            vm(3, TX // VPK, TY, LANES), vm(3, TX // VPK, TY, LANES), vm(3, TX // VPK, TY, LANES),
            *[vm(2, *span(way), LANES) for way in WAYS],
            pltpu.SemaphoreType.DMA((COPIES,)), pltpu.SemaphoreType.DMA((COPIES,)),
        ],
        compiler_params=pltpu.CompilerParams(collective_id=0, has_side_effects=True,
                                             vmem_limit_bytes=16 << 20),
    )(*(pltpu.with_memory_space_constraint(x, pltpu.HBM) for x in (velocity, gradients, shift_x, shift_y, shift_z, fractions)))


def solution(mesh):
    in_specs = (
        P(None, "gx", "gy", "gz"),
        P(None, None, "gx", "gy", "gz"),
        P(None, "gx", "gy", "gz"),
        P(None, "gx", "gy", "gz"),
        P(None, "gx", "gy", "gz"),
        P(None, None, "gx", "gy", "gz"),
    )
    out_specs = P(None, "gx", "gy", "gz")
    return jax.shard_map(functools.partial(body, dict(mesh.shape)), mesh=mesh, in_specs=in_specs,
                         out_specs=out_specs, check_vma=False)
```

profile of v0, /device:TPU:0, one launch (start us, length us, event | category | flops | bytes accessed | tf_op | source)
XLA Modules:
  0.0 29.7 jit_solution(12661072024852208375)
XLA Ops:
  0.0 28.9 %shard_map.64 = f32[3,16,16,128]{3,2,1,0:T(8,128)S(1)} custom-call(f32[3,16,16,128]{3,2,1,0:T(8,128)} %vel_in.1, bf16[2,3,16,16,128]{4,3,2,1,0:T(8,128)(2,1)} %grad_in.1, s32[2,2,1,2]{3,2,1,0:T(1,128)} %bitcast.11, s32[2,2,1,2]{3,2,1,0:T(1,128)} %bitcast.12, s32[2,2,1,2]{3,2,1,0:T(1,128)} %bitcast.13, s32[2,2,2,1,3]{4,3,2,1,0:T(1,128)} %bitcast.10), custom_call_target="tpu_custom_call" | custom-call | tf_op jit(solution)/shard_map/pallas_call | solution.py:392
  28.9 0.7 %copy.11 = f32[3,16,16,128]{3,2,1,0:T(8,128)} copy(f32[3,16,16,128]{3,2,1,0:T(8,128)S(1)} %shard_map.64) | data formatting | bytes 786432
where the time goes:
time: 29.8 us; the launch traced here: 29.7 us
  Pallas kernels  28.9 us (97%)
  local copies, waits for them, and re-layouts  0.75 us (3%)
    pallas_call x1, Pallas kernels, body(): pl.pallas_call(functools.partial(kernel, shape), out_shape=jax.ShapeDtype...  28.9 us
    unnamed x1, local copies, waits for them, and re-layouts  0.75 us

commit v1 on v0

v1 whole, which is shorter than its diff:
```python
import functools

import jax
import jax.numpy as jnp
from jax import lax
from jax.experimental import pallas as pl
from jax.experimental.pallas import tpu as pltpu
from jax.sharding import PartitionSpec as P

BX = 8
BY = 8
BZ = 128
RX = 6
RY = 6
RZ = 14
STEPS = 2

STEP_SIZE = 0.5
REG_WEIGHT = 0.1
LAPLACE_TAPS = (-205.0 / 72.0, 8.0 / 5.0, -1.0 / 5.0, 8.0 / 315.0, -1.0 / 560.0)

HX = RX + 2
HY = RY + 2
HZ = RZ + 2
LANES = 128
PK = LANES // HZ
XG = HX // PK
LH = 4
VPK = LANES // (2 * LH)
WX = BX + 2 * HX
WY = BY + 2 * HY
TILE = 8
MESH = pl.DeviceIdType.MESH
AXES = ("gx", "gy", "gz")
WAYS = sorted(((i, j, k) for i in (-1, 0, 1) for j in (-1, 0, 1) for k in (-1, 0, 1) if (i, j, k) != (0, 0, 0)),
              key=lambda d: (not d[0], sum(map(abs, d))))


def piece(way, own, halo):
    return {-1: (0, halo), 0: (halo, halo + own), 1: (halo + own, 2 * halo + own)}[way]


def border(way, own, halo):
    return {-1: (halo, 2 * halo), 0: (halo, halo + own), 1: (own, halo + own)}[way]


def kernel(shape, vel_in, grad_in, shx_in, shy_in, shz_in, frac_in, out,
           vel, grad, shx, shy, shz, frac, arrive,
           E0, E1, LX, U, YP, XP, ACC0, ACC1, BK0, BK1, ADJ, SP,
           VE, YSU, YSD, YVD, YVU, SV, VRD, VRU, BULK, send, recv):
    TX, TY, TZ = vel.shape[1:]
    NBX, NBY = TX // BX, TY // BY
    EX = TX + 2 * HX
    EY = TY + 2 * HY
    EG = EX // PK
    G = TX // PK
    OX = slice(HX, HX + TX)
    OY = slice(HY, HY + TY)
    NT = TY // TILE

    at = {a: lax.axis_index(a) for a in AXES}

    def has(way):
        ok = None
        for a, w in zip(AXES, way):
            if w:
                one = at[a] < shape[a] - 1 if w > 0 else at[a] > 0
                ok = one if ok is None else jnp.logical_and(ok, one)
        return ok

    def device(way):
        return {a: at[a] + w for a, w in zip(AXES, way) if w}

    up = (at["gx"] == 0).astype(jnp.int32)

    def column(i):
        return i * up + (NBX - 1 - i) * (1 - up)

    def group_of(q):
        return q * up + (EG - 1 - q) * (1 - up)

    loads = []

    def load(src, dst):
        loads.append(pltpu.make_async_copy(src, dst, arrive.at[len(loads)]))
        loads[-1].start()
        return loads[-1]

    def part(ref, i):
        return ref.at[:, pl.ds(column(i) * BX, BX)]

    sources = [(load(part(vel_in, i), part(vel, i)), load(part(grad_in.at[0], i), part(grad.at[0], i)))
               for i in reversed(range(NBX))]
    later = [load(a, b) for a, b in ((shx_in, shx), (shy_in, shy), (shz_in, shz), (frac_in, frac),
                                     (grad_in.at[1], grad.at[1]))]

    barrier = pltpu.get_barrier_semaphore()
    total = jnp.int32(0)
    for way in WAYS:
        @pl.when(has(way))
        def _(way=way):
            pl.semaphore_signal(barrier, inc=1, device_id=device(way), device_id_type=MESH)
        total = total + has(way).astype(jnp.int32)

    def counts(a):
        n = (at[a] > 0).astype(jnp.int32) + (at[a] < shape[a] - 1).astype(jnp.int32)
        return [(v, n == v if shape[a] > 2 else None) for v in ((0,), (1,), (1, 2))[min(shape[a], 3) - 1]]

    def wait_for(sem, tiles, axes, also=None):
        combos = [((), also)]
        for a in axes:
            combos = [(vs + (v,), c if ok is None else ok if c is None else jnp.logical_and(c, ok))
                      for vs, c in combos for v, ok in counts(a)]
        for vs, ok in combos:
            n = tiles(*vs)
            if not n:
                continue
            wait = pltpu.make_async_copy(BULK.at[0:n], BULK.at[0:n], sem).wait
            if ok is None:
                wait()
            else:
                pl.when(ok)(wait)

    def tiles_of(x, y, z):
        return x * y * z // (TILE * LANES)

    def wait_rest(n):
        wait_for(recv.at[3 * n], lambda y, z: tiles_of(TX, TY + HY * y, LANES + HZ * z) - tiles_of(TX, TY, LANES),
                 ("gy", "gz"))

    def wait_x(n, side, also=None):
        ok = has((side, 0, 0))
        wait_for(recv.at[3 * n + (1 if side < 0 else 2)], lambda y, z: tiles_of(HX, TY + HY * y, LANES + HZ * z),
                 ("gy", "gz"), ok if also is None else jnp.logical_and(ok, also))

    def wait_far(n):
        if shape["gx"] > 2:
            wait_x(n, 1, up == 0)

    def wait_near(n):
        wait_x(n, -1)
        wait_x(n, 1, up == 1 if shape["gx"] > 2 else None)

    def wait_sent(n):
        wait_for(send.at[n], lambda x, y, z: tiles_of(TX + HX * x, TY + HY * y, LANES + HZ * z) - tiles_of(TX, TY, LANES),
                 AXES)

    def start(src, dst, way, sent, came):
        desc = pltpu.make_async_remote_copy(
            src_ref=src, dst_ref=dst, send_sem=send.at[sent], recv_sem=recv.at[came],
            device_id=device(way), device_id_type=MESH)
        pl.when(has(way))(desc.start)

    lane2 = lax.broadcasted_iota(jnp.int32, (1, LANES), 1)
    group = lane2 // HZ
    edge = jnp.logical_or(lane2 < HZ, lane2 >= LANES - HZ)

    def packed(layer):
        first = last = None
        for j in range(PK):
            turned = pltpu.roll(layer(j), HZ * j, 1) if j else layer(0)
            first = turned if j == 0 else jnp.where(group == j, turned, first)
            last = turned if j == 0 else jnp.where(group == j - 1, turned, last)
        return first, last

    def unpacked(first, last, j):
        both = jnp.where(group == j, first, last)
        return pltpu.roll(both, LANES - HZ * j, 1) if j else both

    def region(way, dim_of):
        (x0, x1) = dim_of(way[0], G if way[2] else TX, XG if way[2] else HX)
        (y0, y1) = dim_of(way[1], TY, HY)
        return slice(x0, x1), slice(y0, y1)

    def rim(ref, way):
        xs, ys = region(way, piece)
        base = {0: 0, -1: EX, 1: EX + EG}[way[2]]
        return ref.at[slice(base + xs.start, base + xs.stop), ys, :]

    def landing(k, way):
        x = {0: slice(0, HX), -1: slice(HX, HX + XG), 1: slice(HX + XG, HX + 2 * XG)}[way[2]]
        return LX.at[k, (way[0] + 1) // 2, x, region(way, piece)[1], :]

    def forward_send(E, k, n, ways):
        for way in ways:
            xs, ys = region(way, border)
            src = SP.at[k, 0 if way[2] < 0 else 1, xs, ys, :] if way[2] else E.at[xs, ys, :]
            other = tuple(-w for w in way)
            start(src, landing(k, other) if way[0] else rim(E, other), way, n, 3 * n + (0, 1, 2)[way[0]])

    def return_send(ACC, BK, n, ways):
        for way in ways:
            other = tuple(-w for w in way)
            start(rim(ACC, way), rim(BK, other), way, n, 3 * n + (0, 1, 2)[way[0]])

    X_WAYS = [w for w in WAYS if w[0]]
    REST = [w for w in WAYS if not w[0]]

    def pack_column(E, k, bx):
        SP[k, 0, XG + bx, OY, :], SP[k, 1, XG + bx, OY, :] = packed(lambda j: E[HX + bx * BX + j, OY, :])

    def unpack(below, above, g):
        for j in range(PK):
            U[PK * g + j] = unpacked(above, below, j)

    def taps(k, d, bx, by):
        e = frac[k, bx, by, 0, d].astype(jnp.float32) * 0.125
        e2 = e * e
        e3 = e2 * e
        return (0.5 * (2.0 * e2 - e3 - e), 0.5 * (3.0 * e3 - 5.0 * e2 + 2.0),
                0.5 * (4.0 * e2 - 3.0 * e3 + e), 0.5 * (e3 - e2))

    def total_of(terms):
        return functools.reduce(lambda a, b: a + b, terms)

    def gather_block(E, k, bx, by):
        a, b, c = shx[k, bx, 0, by], shy[k, bx, 0, by], shz[k, bx, 0, by]
        wx, wy, wz = (taps(k, d, bx, by) for d in range(3))
        x0 = bx * BX + (a + HX - 1)
        y0 = by * BY + (b + HY - 1)
        along = []
        for ref in (E, U):
            rows = [total_of(wy[v] * ref[x0 + m, pl.ds(y0 + v, BY), :] for v in range(4)) for m in range(BX + 3)]
            along.append([total_of(wx[u] * rows[m + u] for u in range(4)) for m in range(BX)])
        own, rest = (jnp.concatenate(p, axis=0) for p in along)
        res = None
        for w in range(4):
            s = c + (w - 1)
            inside = jnp.logical_and(lane2 >= s, lane2 < LANES + s)
            term = wz[w] * pltpu.roll(jnp.where(inside, own, rest), lax.rem(LANES - s, LANES), 1)
            res = term if res is None else res + term
        return [res[BY * m:BY * (m + 1)] for m in range(BX)]

    def spread_block(vals, k, i, bx, by):
        n = i * NBY + by
        c = shz[k, bx, 0, by]
        wx, wy, wz = (taps(k, d, bx, by) for d in range(3))
        flat = jnp.concatenate(vals, axis=0)
        own = rest = None
        for w in range(4):
            s = c + (w - 1)
            inside = jnp.logical_and(lane2 >= s, lane2 < LANES + s)
            term = wz[w] * pltpu.roll(flat, lax.rem(LANES + s, LANES), 1)
            o, r = jnp.where(inside, term, 0.0), jnp.where(inside, 0.0, term)
            own, rest = (o, r) if own is None else (own + o, rest + r)
        for p, zs in enumerate((own, rest)):
            z = [zs[BY * m:BY * (m + 1)] for m in range(BX)]
            for m in range(BX + 3):
                YP[n, p, m, TILE:TILE + BY, :] = total_of(wx[u] * z[m - u] for u in range(4) if 0 <= m - u < BX)
            for m in range(BX + 3):
                XP[n, p, 2 * HX + m, 2 * TILE:2 * TILE + 2 * BY, :] = total_of(
                    wy[v] * YP[n, p, m, TILE - v:TILE - v + 2 * BY, :] for v in range(4))

    def collect(ACC, k, q):
        g = group_of(q)
        found = []
        for i in range(NBX):
            if 0 <= q - i <= 2:
                bx = column(i)
                offset = BX * ((q - i) * up + (2 - q + i) * (1 - up))
                for by in range(NBY):
                    found.append((i * NBY + by, by, (HX + 1) - shx[k, bx, 0, by] + offset,
                                  (2 * TILE - HY + 1) - shy[k, bx, 0, by]))

        def layer(p, j):
            tiles = [None] * (EY // TILE)
            for n, by, x0, y0 in found:
                rows = XP[n, p, x0 + j, pl.ds(y0, WY), :]
                for r in range(WY // TILE):
                    one = rows[r * TILE:(r + 1) * TILE]
                    old = tiles[by + r]
                    tiles[by + r] = one if old is None else old + one
            return jnp.concatenate(tiles, axis=0)

        for j in range(PK):
            ACC[PK * g + j] = layer(0, j)
        rims = [layer(1, j) for j in range(PK)]
        ACC[EX + EG + g], ACC[EX + g] = packed(lambda j: rims[j])

    def received(ACC, BK, i):
        bx = column(i)
        halos = ([0] if i == 0 and shape["gx"] > 2 else []) + ([EG - 1] if i == NBX - 1 else [])
        halos = [group_of(q) for q in halos]

        def rows(center, L):
            tiles = [center[L, HY + TILE * t:HY + TILE * (t + 1), :] for t in range(NT)]
            tiles[0] = tiles[0] + BK[L, 0:HY, :]
            tiles[-1] = tiles[-1] + BK[L, HY + TY:, :]
            return jnp.concatenate(tiles, axis=0)

        rims = []
        for base in (EX, EX + EG):
            rims.append(total_of([rows(BK, base + XG + bx)] + [rows(BK, base + g) for g in halos]))
        first, last = rims
        res = []
        for j in range(BX):
            one = total_of([rows(ACC, HX + bx * BX + j)] + [rows(BK, PK * g + j) for g in halos])
            res.append(one + jnp.where(edge, unpacked(first, last, j), 0.0))
        return res

    def blocks(layers, by):
        return [one[by * BY:(by + 1) * BY] for one in layers]

    def product(k, bx, j):
        return STEP_SIZE * total_of(grad[k, c, bx * BX + j].astype(jnp.float32) * vel[c, bx * BX + j] for c in range(3))

    def clear(a, first, last):
        for end, views in ((0, first), (shape[a] - 1, last)):
            @pl.when(at[a] == end)
            def _(views=views):
                for ref in views:
                    ref[...] = jnp.zeros_like(ref)

    def clear_missing():
        sides = ((slice(0, HX), slice(EX, EX + XG), slice(EX + EG, EX + EG + XG)),
                 (slice(HX + TX, EX), slice(EX + XG + G, EX + EG), slice(EX + EG + XG + G, EX + 2 * EG)))
        low, high = ([BK.at[x] for BK in (BK0, BK1) for x in side] for side in sides)
        clear("gx", low + [LX.at[:, 0], VE.at[:, 0:LH]], high + [LX.at[:, 1], VE.at[:, LH + TX:]])
        ends = slice(0, HY), slice(HY + TY, EY)
        low, high = ([ref.at[:, y] for ref in (E0, E1, BK0, BK1)] + [LX.at[:, :, :, y]] for y in ends)
        clear("gy", low + [YVD], high + [YVU])
        low, high = ([ref.at[x] for ref in (E0, E1, BK0, BK1)] for x in (slice(EX, EX + EG), slice(EX + EG, EX + 2 * EG)))
        clear("gz", low + [LX.at[:, :, HX:HX + XG], VRD], high + [LX.at[:, :, HX + XG:], VRU])

    def send_faces():
        n = 4
        copies = [((1, 0, 0), vel.at[:, TX - LH:TX], VE.at[:, 0:LH, OY, :]),
                  ((-1, 0, 0), vel.at[:, 0:LH], VE.at[:, LH + TX:2 * LH + TX, OY, :])]
        for way, src, dst in copies:
            start(src, dst, way, n, 3 * n)
        VE[:, LH:LH + TX, OY, :] = vel[...]
        for c in range(3):
            for i in range(TX // 2):
                for h in range(2):
                    YSU[c, i, LH * h:LH * (h + 1), :] = vel[c, 2 * i + h, TY - LH:TY, :]
                    YSD[c, i, LH * h:LH * (h + 1), :] = vel[c, 2 * i + h, 0:LH, :]
            for g in range(TX // VPK):
                row = None
                for j in range(VPK):
                    turned = pltpu.roll(vel[c, VPK * g + j], (2 * LH * j + LH) % LANES, 1)
                    row = turned if row is None else jnp.where(lane2 // (2 * LH) == j, turned, row)
                SV[c, g] = row
        for way, src, dst in (((0, 1, 0), YSU, YVD), ((0, -1, 0), YSD, YVU),
                              ((0, 0, 1), SV, VRD), ((0, 0, -1), SV, VRU)):
            start(src, dst, way, n, 3 * n)

    def face_tiles(x, y, z):
        return (x * tiles_of(3 * LH, TY, LANES) + y * tiles_of(3 * TX // 2, 2 * LH, LANES)
                + z * tiles_of(3 * TX // VPK, TY, LANES))

    def regular():
        wait_for(recv.at[12], face_tiles, AXES)
        for c in range(3):
            for i in range(TX // 2):
                for h in range(2):
                    VE[c, LH + 2 * i + h, HY - LH:HY, :] = YVD[c, i, LH * h:LH * (h + 1), :]
                    VE[c, LH + 2 * i + h, HY + TY:HY + TY + LH, :] = YVU[c, i, LH * h:LH * (h + 1), :]
        rows = lax.broadcasted_iota(jnp.int32, (2 * LANES, LANES), 0)
        cols = lax.broadcasted_iota(jnp.int32, (2 * LANES, LANES), 1)
        r = rows - LANES
        place = jnp.where(rows < LANES, rows, jnp.where(r < LH, r + LANES, r - LANES))
        known = jnp.logical_or(rows < LANES, jnp.logical_or(r < LH, r >= LANES - LH))
        gap = jnp.abs(place - cols)
        band = jnp.zeros((2 * LANES, LANES), jnp.float32)
        for k in range(5):
            tap = (3.0 if k == 0 else 1.0) * LAPLACE_TAPS[k]
            band = jnp.where(jnp.logical_and(known, gap == k), tap, band)
        for c in range(3):
            rims = []
            for g in range(TX // VPK):
                row = jnp.where(lane2 % (2 * LH) < LH, VRD[c, g], VRU[c, g])
                for j in range(VPK):
                    rims.append(pltpu.roll(row, (LANES - (2 * LH * j + LH)) % LANES, 1))
            rims = jnp.concatenate(rims, axis=0)
            own = vel[c].reshape(TX * TY, LANES)
            res = jnp.dot(jnp.concatenate([own, rims], axis=1), band,
                          preferred_element_type=jnp.float32,
                          precision=lax.Precision.HIGHEST).reshape(TX, TY, LANES)
            for k in range(1, 5):
                res = res + LAPLACE_TAPS[k] * (
                    VE[c, LH + k:LH + k + TX, OY, :] + VE[c, LH - k:LH - k + TX, OY, :]
                    + VE[c, LH:LH + TX, HY + k:HY + k + TY, :]
                    + VE[c, LH:LH + TX, HY - k:HY - k + TY, :])
            out[c] = (-REG_WEIGHT) * res

    met = False
    for i in reversed(range(NBX)):
        for copy in sources[NBX - 1 - i]:
            copy.wait()
        bx = column(i)
        for j in range(BX):
            E0[HX + bx * BX + j, OY, :] = product(0, bx, j)
        pack_column(E0, 0, bx)
        if not met and (i == NBX - 1 and shape["gx"] <= 2 or i == 0):
            pl.semaphore_wait(barrier, total)
            forward_send(E0, 0, 0, X_WAYS)
            met = True
    forward_send(E0, 0, 0, REST)

    clear_missing()
    send_faces()
    for copy in later:
        copy.wait()
    for i in range(NBX):
        for j in range(BX):
            E1[HX + column(i) * BX + j, OY, :] = product(1, column(i), j)
    YP[:, :, :, 0:TILE] = jnp.zeros_like(YP[:, :, :, 0:TILE])
    YP[:, :, :, TILE + BY:] = jnp.zeros_like(YP[:, :, :, TILE + BY:])
    XP[...] = jnp.zeros_like(XP)

    def enter(E, k, g, side):
        for j in range(HX):
            E[PK * g + j] = LX[k, side, j]
        unpack(LX[k, side, HX], LX[k, side, HX + XG], g)

    def forward(E, n, each):
        wait_rest(n)
        for i in range(NBX):
            g = XG + column(i)
            unpack(E[EX + g], E[EX + EG + g], g)
        for i in range(NBX):
            if i == 0:
                wait_far(n)
                enter(E, n, group_of(0), 1 - up)
            if i == NBX - 1:
                wait_near(n)
                enter(E, n, group_of(EG - 1), up)
            each(i, column(i))

    def first(i, bx):
        for by in range(NBY):
            res = gather_block(E0, 0, bx, by)
            for m in range(BX):
                rows = slice(HY + by * BY, HY + (by + 1) * BY)
                E1[HX + bx * BX + m, rows, :] = E1[HX + bx * BX + m, rows, :] + res[m]
        pack_column(E1, 1, bx)

    forward(E0, 0, first)
    forward_send(E1, 1, 1, X_WAYS)
    forward_send(E1, 1, 1, REST)

    def second(i, bx):
        for by in range(NBY):
            spread_block(gather_block(E1, 1, bx, by), 1, i, bx, by)

    forward(E1, 1, second)

    def give_back(ACC, BK, k, n):
        collect(ACC, k, EG - 1)
        if shape["gx"] > 2:
            collect(ACC, k, 0)
        return_send(ACC, BK, n, X_WAYS)
        for q in range(XG, XG + G):
            collect(ACC, k, q)
        return_send(ACC, BK, n, REST)

    def backward(ACC, BK, n, each):
        wait_rest(n)
        for i in range(NBX):
            if i == 0:
                wait_far(n)
            if i == NBX - 1:
                wait_near(n)
            each(i, column(i), received(ACC, BK, i))

    give_back(ACC1, BK1, 1, 2)
    regular()

    def third(i, bx, layers):
        for j in range(BX):
            ADJ[bx * BX + j] = layers[j]
        for by in range(NBY):
            spread_block(blocks(layers, by), 0, i, bx, by)

    backward(ACC1, BK1, 2, third)
    give_back(ACC0, BK0, 0, 3)

    for c in range(3):
        out[c] = out[c] + STEP_SIZE * grad[1, c].astype(jnp.float32) * ADJ[...]
    for n in range(3):
        wait_sent(n)
    wait_for(send.at[4], face_tiles, AXES)

    def fourth(i, bx, layers):
        for c in range(3):
            for j in range(BX):
                x = bx * BX + j
                out[c, x] = out[c, x] + STEP_SIZE * grad[0, c, x].astype(jnp.float32) * layers[j]

    backward(ACC0, BK0, 3, fourth)
    wait_sent(3)


def body(shape, velocity, gradients, shift_x, shift_y, shift_z, fractions):
    TX, TY, TZ = velocity.shape[1:]
    assert TZ == BZ == LANES and TX % VPK == 0 and TX % BX == 0 and TY % BY == 0
    assert BX == HX == PK and BY == HY == TILE and XG == 1
    EX, EY = TX + 2 * HX, TY + 2 * HY
    EG = EX // PK
    NB = (TX // BX) * (TY // BY)
    most = EX * EY * (LANES + 2 * HZ) // (TILE * LANES)

    vm = lambda *s: pltpu.VMEM(s, jnp.float32)
    vmem = pl.BlockSpec(memory_space=pltpu.VMEM)
    hbm = pl.BlockSpec(memory_space=pltpu.HBM)
    shift_x, shift_y, shift_z = (s.transpose(0, 1, 3, 2) for s in (shift_x, shift_y, shift_z))
    fractions = fractions.transpose(0, 2, 3, 4, 1)
    return pl.pallas_call(
        functools.partial(kernel, shape),
        out_shape=jax.ShapeDtypeStruct(velocity.shape, jnp.float32),
        in_specs=[hbm] * 6,
        out_specs=vmem,
        scratch_shapes=[
            pltpu.VMEM(velocity.shape, velocity.dtype), pltpu.VMEM(gradients.shape, gradients.dtype),
            *[pltpu.SMEM(s.shape, s.dtype) for s in (shift_x, shift_y, shift_z, fractions)],
            pltpu.SemaphoreType.DMA((2 * (TX // BX) + 5,)),
            vm(EX + 2 * EG, EY, LANES), vm(EX + 2 * EG, EY, LANES),
            vm(2, 2, HX + 2 * XG, EY, LANES), vm(EX, EY, LANES),
            vm(NB, 2, BX + 3, 3 * TILE, LANES), vm(NB, 2, 2 * WX - BX, 5 * TILE, LANES),
            *[vm(EX + 2 * EG, EY, LANES) for _ in range(4)],
            vm(TX, TY, LANES),
            vm(2, 2, EG, EY, LANES),
            vm(3, TX + 2 * LH, EY, LANES),
            vm(3, TX // 2, 2 * LH, LANES), vm(3, TX // 2, 2 * LH, LANES),
            vm(3, TX // 2, 2 * LH, LANES), vm(3, TX // 2, 2 * LH, LANES),
            vm(3, TX // VPK, TY, LANES), vm(3, TX // VPK, TY, LANES), vm(3, TX // VPK, TY, LANES),
            vm(most, TILE, LANES),
            pltpu.SemaphoreType.DMA((5,)), pltpu.SemaphoreType.DMA((13,)),
        ],
        compiler_params=pltpu.CompilerParams(collective_id=0, has_side_effects=True,
                                             vmem_limit_bytes=24 << 20),
    )(*(pltpu.with_memory_space_constraint(x, pltpu.HBM) for x in (velocity, gradients, shift_x, shift_y, shift_z, fractions)))


def solution(mesh):
    in_specs = (
        P(None, "gx", "gy", "gz"),
        P(None, None, "gx", "gy", "gz"),
        P(None, "gx", "gy", "gz"),
        P(None, "gx", "gy", "gz"),
        P(None, "gx", "gy", "gz"),
        P(None, None, "gx", "gy", "gz"),
    )
    out_specs = P(None, "gx", "gy", "gz")
    return jax.shard_map(functools.partial(body, dict(mesh.shape)), mesh=mesh, in_specs=in_specs,
                         out_specs=out_specs, check_vma=False)
```

time: 29.8 us -> 26.2 us (0.88)
  Pallas kernels: 28.9 us -> 25.3 us
    pallas_call x1, Pallas kernels: 28.9 us -> 25.3 us  [body(): pl.pallas_call(functools.partial(kernel, shape), out_shape=jax.ShapeDtype...]
where the time goes in v1:
time: 26.2 us; the launch traced here: 26.1 us
  Pallas kernels  25.3 us (97%)
  local copies, waits for them, and re-layouts  0.75 us (3%)
    pallas_call x1, Pallas kernels, body(): pl.pallas_call(functools.partial(kernel, shape), out_shape=jax.ShapeDtype...  25.3 us
    unnamed x1, local copies, waits for them, and re-layouts  0.75 us

profile of v1, /device:TPU:0, one launch (start us, length us, event | category | flops | bytes accessed | tf_op | source)
XLA Modules:
  0.0 26.1 jit_solution(534139271757567221)
XLA Ops:
  0.0 25.3 %shard_map.64 = f32[3,16,16,128]{3,2,1,0:T(8,128)S(1)} custom-call(f32[3,16,16,128]{3,2,1,0:T(8,128)} %vel_in.1, bf16[2,3,16,16,128]{4,3,2,1,0:T(8,128)(2,1)} %grad_in.1, s32[2,2,1,2]{3,2,1,0:T(1,128)} %bitcast.11, s32[2,2,1,2]{3,2,1,0:T(1,128)} %bitcast.12, s32[2,2,1,2]{3,2,1,0:T(1,128)} %bitcast.13, s32[2,2,2,1,3]{4,3,2,1,0:T(1,128)} %bitcast.10), custom_call_target="tpu_custom_call" | custom-call | tf_op jit(solution)/shard_map/pallas_call | solution.py:508
  25.3 0.7 %copy.11 = f32[3,16,16,128]{3,2,1,0:T(8,128)} copy(f32[3,16,16,128]{3,2,1,0:T(8,128)S(1)} %shard_map.64) | data formatting | bytes 786432

commit v2 on v1

--- a/solution.py
+++ b/solution.py
@@ -46,7 +46,7 @@
 
 def kernel(shape, vel_in, grad_in, shx_in, shy_in, shz_in, frac_in, out,
            vel, grad, shx, shy, shz, frac, arrive,
-           E0, E1, LX, U, YP, XP, ACC0, ACC1, BK0, BK1, ADJ, SP,
+           E0, E1, LX, HA, RL, U, YP, XP, ACC0, ACC1, BK0, BK1, ADJ, SP,
            VE, YSU, YSD, YVD, YVU, SV, VRD, VRU, BULK, send, recv):
     TX, TY, TZ = vel.shape[1:]
     NBX, NBY = TX // BX, TY // BY
@@ -73,6 +73,22 @@
 
     up = (at["gx"] == 0).astype(jnp.int32)
 
+    NS = 2 if shape["gx"] > 2 else 1
+    even = 1 - lax.rem(at["gy"], 2)
+    off = jnp.where(even == 1, at["gy"] > 0, at["gy"] < shape["gy"] - 1)
+
+    def place(h):
+        return h if NS == 2 else 0
+
+    def multiple(x):
+        return pl.multiple_of(x, TILE)
+
+    A = pl.ds(multiple(HY + even * (TY - HY)), HY)
+    B = pl.ds(multiple(HY + (1 - even) * HY), TY - HY)
+    OFF = pl.ds(multiple(HY + (1 - even) * (TY - HY)), HY)
+    INNER = pl.ds(multiple(even * (HY + TY)), HY)
+    OUTER = pl.ds(multiple((1 - even) * (HY + TY)), HY)
+
     def column(i):
         return i * up + (NBX - 1 - i) * (1 - up)
 
@@ -103,6 +119,8 @@
         total = total + has(way).astype(jnp.int32)
 
     def counts(a):
+        if a == "off":
+            return [(v, off if v else jnp.logical_not(off)) for v in range(2)] if shape["gy"] > 2 else [(0, None)]
         n = (at[a] > 0).astype(jnp.int32) + (at[a] < shape[a] - 1).astype(jnp.int32)
         return [(v, n == v if shape[a] > 2 else None) for v in ((0,), (1,), (1, 2))[min(shape[a], 3) - 1]]
 
@@ -124,32 +142,64 @@
     def tiles_of(x, y, z):
         return x * y * z // (TILE * LANES)
 
+    EACH = 1 + 2 * NS
+    SIDES = [] if shape["gx"] == 1 else [(up, None)] if NS == 1 else [(0, has((-1, 0, 0))), (1, has((1, 0, 0)))]
+
     def wait_rest(n):
-        wait_for(recv.at[3 * n], lambda y, z: tiles_of(TX, TY + HY * y, LANES + HZ * z) - tiles_of(TX, TY, LANES),
+        wait_for(recv.at[EACH * n], lambda y, z: tiles_of(TX, TY + HY * y, LANES + HZ * z) - tiles_of(TX, TY, LANES),
                  ("gy", "gz"))
 
-    def wait_x(n, side, also=None):
-        ok = has((side, 0, 0))
-        wait_for(recv.at[3 * n + (1 if side < 0 else 2)], lambda y, z: tiles_of(HX, TY + HY * y, LANES + HZ * z),
-                 ("gy", "gz"), ok if also is None else jnp.logical_and(ok, also))
-
-    def wait_far(n):
-        if shape["gx"] > 2:
-            wait_x(n, 1, up == 0)
-
-    def wait_near(n):
-        wait_x(n, -1)
-        wait_x(n, 1, up == 1 if shape["gx"] > 2 else None)
+    def wait_early(n, h, ok):
+        wait_for(recv.at[EACH * n + 1 + place(h)], lambda z: tiles_of(HX, HY, LANES) + tiles_of(HX, TY, HZ * z), ("gz",), ok)
+
+    def wait_late(n, h, ok):
+        wait_for(recv.at[EACH * n + 1 + NS + place(h)], lambda y, z: tiles_of(HX, TY - HY, LANES)
+                 + tiles_of(HX + 2 * XG, HY, LANES) + y * tiles_of(HX, HY, LANES + HZ * z), ("off", "gz"), ok)
+
+    def wait_back(n, h, ok):
+        wait_for(recv.at[EACH * n + 1 + place(h)], lambda y, z: tiles_of(HX, TY + HY * y, LANES + HZ * z), ("off", "gz"), ok)
+
+    def wait_pair(n, h, ok):
+        wait_for(recv.at[EACH * n + 1 + NS + place(h)], lambda: tiles_of(HX + 2 * XG, HY, LANES), (), ok)
+
+    def far_of(wait, n):
+        if NS == 2:
+            wait(n, 1, jnp.logical_and(SIDES[1][1], up == 0))
+
+    def near_of(wait, n):
+        for h, ok in SIDES:
+            wait(n, h, jnp.logical_and(ok, up == 1) if NS == 2 and h else ok)
 
     def wait_sent(n):
-        wait_for(send.at[n], lambda x, y, z: tiles_of(TX + HX * x, TY + HY * y, LANES + HZ * z) - tiles_of(TX, TY, LANES),
-                 AXES)
+        wait_for(send.at[n], lambda x, y, z: tiles_of(TX, TY + HY * (1 + y), LANES + HZ * z) - tiles_of(TX, TY, LANES)
+                 + x * (tiles_of(HX, TY + HY * y, LANES + HZ * z) + tiles_of(HX + 2 * XG, HY, LANES)),
+                 ("gx", "off", "gz"))
 
     def start(src, dst, way, sent, came):
+        to_device(src, dst, device(way), has(way), sent, came)
+
+    def to_device(src, dst, where, ok, sent, came):
         desc = pltpu.make_async_remote_copy(
             src_ref=src, dst_ref=dst, send_sem=send.at[sent], recv_sem=recv.at[came],
-            device_id=device(way), device_id_type=MESH)
-        pl.when(has(way))(desc.start)
+            device_id=where, device_id_type=MESH)
+        if ok is None:
+            desc.start()
+        else:
+            pl.when(ok)(desc.start)
+
+    def both(*oks):
+        oks = [ok for ok in oks if ok is not None]
+        return functools.reduce(jnp.logical_and, oks) if oks else None
+
+    def beside(h, y=0, z=0):
+        where = {"gx": at["gx"] + 2 * h - 1}
+        if y:
+            where["gy"] = at["gy"] + (1 - 2 * even if y < 0 else 2 * even - 1)
+        if z:
+            where["gz"] = at["gz"] + z
+        return where
+
+    partner = {"gy": at["gy"] + 2 * even - 1}
 
     lane2 = lax.broadcasted_iota(jnp.int32, (1, LANES), 1)
     group = lane2 // HZ
@@ -177,23 +227,58 @@
         base = {0: 0, -1: EX, 1: EX + EG}[way[2]]
         return ref.at[slice(base + xs.start, base + xs.stop), ys, :]
 
-    def landing(k, way):
-        x = {0: slice(0, HX), -1: slice(HX, HX + XG), 1: slice(HX + XG, HX + 2 * XG)}[way[2]]
-        return LX.at[k, (way[0] + 1) // 2, x, region(way, piece)[1], :]
-
-    def forward_send(E, k, n, ways):
-        for way in ways:
+    def forward_x(E, k, n):
+        for h, ok in SIDES:
+            mine, g, into = pl.ds(HX + h * (TX - HX), HX), XG + h * (G - XG), LX.at[k, place(1 - h)]
+            early, late = EACH * n + 1 + place(1 - h), EACH * n + 1 + NS + place(1 - h)
+            to_device(E.at[mine, A, :], into.at[0:HX, A, :], beside(h), ok, n, early)
+            for z in (-1, 1):
+                to_device(SP.at[k, (z + 1) // 2, g, OY, :], into.at[HX + (1 - z) // 2, OY, :],
+                          beside(h, 0, z), both(ok, has((0, 0, z))), n, early)
+            to_device(E.at[mine, OFF, :], into.at[0:HX, INNER, :], beside(h, -1), both(ok, off), n, late)
+            for z in (-1, 1):
+                to_device(SP.at[k, (z + 1) // 2, g, OFF, :], into.at[HX + (1 - z) // 2, INNER, :],
+                          beside(h, -1, z), both(ok, off, has((0, 0, z))), n, late)
+            to_device(E.at[mine, B, :], into.at[0:HX, B, :], beside(h), ok, n, late)
+
+    def forward_pair(k, n):
+        for h, ok in SIDES:
+            wait_early(n, h, ok)
+            to_device(LX.at[k, place(h), :, A, :], LX.at[k, place(h), :, OUTER, :], partner, ok, n,
+                      EACH * n + 1 + NS + place(h))
+
+    def forward_rest(E, k, n):
+        for way in REST:
             xs, ys = region(way, border)
             src = SP.at[k, 0 if way[2] < 0 else 1, xs, ys, :] if way[2] else E.at[xs, ys, :]
-            other = tuple(-w for w in way)
-            start(src, landing(k, other) if way[0] else rim(E, other), way, n, 3 * n + (0, 1, 2)[way[0]])
-
-    def return_send(ACC, BK, n, ways):
-        for way in ways:
-            other = tuple(-w for w in way)
-            start(rim(ACC, way), rim(BK, other), way, n, 3 * n + (0, 1, 2)[way[0]])
-
-    X_WAYS = [w for w in WAYS if w[0]]
+            start(src, rim(E, tuple(-w for w in way)), way, n, EACH * n)
+
+    def return_x(k, BK, n, part):
+        for h, ok in SIDES:
+            mine, came = HA.at[k, place(h)], EACH * n + 1 + place(1 - h)
+            first = (1 - h) * (HX + TX)
+            g = (1 - h) * (EG - 1)
+
+            def send_rows(rows, into, y, ok):
+                to_device(mine.at[0:HX, rows, :], BK.at[pl.ds(first, HX), into, :], beside(h, y), ok, n, came)
+                for z in (-1, 1):
+                    to_device(mine.at[HX + (z + 1) // 2, rows, :], BK.at[EX + EG * ((1 - z) // 2) + g, into, :],
+                              beside(h, y, z), both(ok, has((0, 0, z))), n, came)
+
+            if part == 0:
+                to_device(mine.at[:, INNER, :], RL.at[k, place(h)], partner, ok, n, EACH * n + 1 + NS + place(h))
+                send_rows(OUTER, INNER, -1, both(ok, off))
+                send_rows(B, B, 0, ok)
+            else:
+                wait_pair(n, h, ok)
+                for L in range(HX + 2 * XG):
+                    HA[k, place(h), L, A, :] = HA[k, place(h), L, A, :] + RL[k, place(h), L]
+                send_rows(A, A, 0, ok)
+
+    def return_rest(ACC, BK, n):
+        for way in REST:
+            start(rim(ACC, way), rim(BK, tuple(-w for w in way)), way, n, EACH * n)
+
     REST = [w for w in WAYS if not w[0]]
 
     def pack_column(E, k, bx):
@@ -251,7 +336,7 @@
                 XP[n, p, 2 * HX + m, 2 * TILE:2 * TILE + 2 * BY, :] = total_of(
                     wy[v] * YP[n, p, m, TILE - v:TILE - v + 2 * BY, :] for v in range(4))
 
-    def collect(ACC, k, q):
+    def collect(k, q, ACC=None, halo=None):
         g = group_of(q)
         found = []
         for i in range(NBX):
@@ -272,14 +357,21 @@
                     tiles[by + r] = one if old is None else old + one
             return jnp.concatenate(tiles, axis=0)
 
+        rims = [layer(1, j) for j in range(PK)]
+        above, below = packed(lambda j: rims[j])
         for j in range(PK):
-            ACC[PK * g + j] = layer(0, j)
-        rims = [layer(1, j) for j in range(PK)]
-        ACC[EX + EG + g], ACC[EX + g] = packed(lambda j: rims[j])
+            if halo is not None:
+                HA[k, halo, j] = layer(0, j)
+            else:
+                ACC[PK * g + j] = layer(0, j)
+        if halo is not None:
+            HA[k, halo, HX], HA[k, halo, HX + XG] = below, above
+        else:
+            ACC[EX + EG + g], ACC[EX + g] = above, below
 
     def received(ACC, BK, i):
         bx = column(i)
-        halos = ([0] if i == 0 and shape["gx"] > 2 else []) + ([EG - 1] if i == NBX - 1 else [])
+        halos = ([0] if i == 0 and NS == 2 else []) + ([EG - 1] if i == NBX - 1 else [])
         halos = [group_of(q) for q in halos]
 
         def rows(center, L):
@@ -315,19 +407,26 @@
         sides = ((slice(0, HX), slice(EX, EX + XG), slice(EX + EG, EX + EG + XG)),
                  (slice(HX + TX, EX), slice(EX + XG + G, EX + EG), slice(EX + EG + XG + G, EX + 2 * EG)))
         low, high = ([BK.at[x] for BK in (BK0, BK1) for x in side] for side in sides)
-        clear("gx", low + [LX.at[:, 0], VE.at[:, 0:LH]], high + [LX.at[:, 1], VE.at[:, LH + TX:]])
+        if NS == 2:
+            low, high = low + [LX.at[:, 0]], high + [LX.at[:, 1]]
+        clear("gx", low + [E.at[x] for E in (E0, E1) for x in sides[0]] + [VE.at[:, 0:LH]],
+              high + [E.at[x] for E in (E0, E1) for x in sides[1]] + [VE.at[:, LH + TX:]])
+        for BK in (BK0, BK1):
+            for x in sides[0] + sides[1]:
+                BK[x, INNER, :] = jnp.zeros_like(BK[x, INNER, :])
         ends = slice(0, HY), slice(HY + TY, EY)
         low, high = ([ref.at[:, y] for ref in (E0, E1, BK0, BK1)] + [LX.at[:, :, :, y]] for y in ends)
         clear("gy", low + [YVD], high + [YVU])
         low, high = ([ref.at[x] for ref in (E0, E1, BK0, BK1)] for x in (slice(EX, EX + EG), slice(EX + EG, EX + 2 * EG)))
-        clear("gz", low + [LX.at[:, :, HX:HX + XG], VRD], high + [LX.at[:, :, HX + XG:], VRU])
+        clear("gz", low + [LX.at[:, :, HX, y] for y in (OY, OUTER)] + [VRD],
+              high + [LX.at[:, :, HX + XG, y] for y in (OY, OUTER)] + [VRU])
 
     def send_faces():
         n = 4
         copies = [((1, 0, 0), vel.at[:, TX - LH:TX], VE.at[:, 0:LH, OY, :]),
                   ((-1, 0, 0), vel.at[:, 0:LH], VE.at[:, LH + TX:2 * LH + TX, OY, :])]
         for way, src, dst in copies:
-            start(src, dst, way, n, 3 * n)
+            start(src, dst, way, n, EACH * n)
         VE[:, LH:LH + TX, OY, :] = vel[...]
         for c in range(3):
             for i in range(TX // 2):
@@ -342,14 +441,14 @@
                 SV[c, g] = row
         for way, src, dst in (((0, 1, 0), YSU, YVD), ((0, -1, 0), YSD, YVU),
                               ((0, 0, 1), SV, VRD), ((0, 0, -1), SV, VRU)):
-            start(src, dst, way, n, 3 * n)
+            start(src, dst, way, n, EACH * n)
 
     def face_tiles(x, y, z):
         return (x * tiles_of(3 * LH, TY, LANES) + y * tiles_of(3 * TX // 2, 2 * LH, LANES)
                 + z * tiles_of(3 * TX // VPK, TY, LANES))
 
     def regular():
-        wait_for(recv.at[12], face_tiles, AXES)
+        wait_for(recv.at[4 * EACH], face_tiles, AXES)
         for c in range(3):
             for i in range(TX // 2):
                 for h in range(2):
@@ -391,11 +490,11 @@
         for j in range(BX):
             E0[HX + bx * BX + j, OY, :] = product(0, bx, j)
         pack_column(E0, 0, bx)
-        if not met and (i == NBX - 1 and shape["gx"] <= 2 or i == 0):
+        if not met and (i == NBX - 1 and NS == 1 or i == 0):
             pl.semaphore_wait(barrier, total)
-            forward_send(E0, 0, 0, X_WAYS)
+            forward_x(E0, 0, 0)
             met = True
-    forward_send(E0, 0, 0, REST)
+    forward_rest(E0, 0, 0)
 
     clear_missing()
     send_faces()
@@ -414,17 +513,22 @@
         unpack(LX[k, side, HX], LX[k, side, HX + XG], g)
 
     def forward(E, n, each):
+        forward_pair(n, n)
         wait_rest(n)
         for i in range(NBX):
             g = XG + column(i)
             unpack(E[EX + g], E[EX + EG + g], g)
         for i in range(NBX):
             if i == 0:
-                wait_far(n)
-                enter(E, n, group_of(0), 1 - up)
+                g = group_of(0)
+                if NS == 2:
+                    far_of(wait_late, n)
+                    enter(E, n, g, 1 - up)
+                else:
+                    unpack(E[EX + g], E[EX + EG + g], g)
             if i == NBX - 1:
-                wait_near(n)
-                enter(E, n, group_of(EG - 1), up)
+                near_of(wait_late, n)
+                enter(E, n, group_of(EG - 1), place(up))
             each(i, column(i))
 
     def first(i, bx):
@@ -436,8 +540,8 @@
         pack_column(E1, 1, bx)
 
     forward(E0, 0, first)
-    forward_send(E1, 1, 1, X_WAYS)
-    forward_send(E1, 1, 1, REST)
+    forward_x(E1, 1, 1)
+    forward_rest(E1, 1, 1)
 
     def second(i, bx):
         for by in range(NBY):
@@ -445,26 +549,27 @@
 
     forward(E1, 1, second)
 
-    def give_back(ACC, BK, k, n):
-        collect(ACC, k, EG - 1)
-        if shape["gx"] > 2:
-            collect(ACC, k, 0)
-        return_send(ACC, BK, n, X_WAYS)
+    def give_back(ACC, BK, k, n, meanwhile):
+        collect(k, EG - 1, halo=place(up))
+        if NS == 2:
+            collect(k, 0, halo=1 - up)
+        return_x(k, BK, n, 0)
         for q in range(XG, XG + G):
-            collect(ACC, k, q)
-        return_send(ACC, BK, n, REST)
+            collect(k, q, ACC)
+        return_rest(ACC, BK, n)
+        meanwhile()
+        return_x(k, BK, n, 1)
 
     def backward(ACC, BK, n, each):
         wait_rest(n)
         for i in range(NBX):
             if i == 0:
-                wait_far(n)
+                far_of(wait_back, n)
             if i == NBX - 1:
-                wait_near(n)
+                near_of(wait_back, n)
             each(i, column(i), received(ACC, BK, i))
 
-    give_back(ACC1, BK1, 1, 2)
-    regular()
+    give_back(ACC1, BK1, 1, 2, regular)
 
     def third(i, bx, layers):
         for j in range(BX):
@@ -473,13 +578,14 @@
             spread_block(blocks(layers, by), 0, i, bx, by)
 
     backward(ACC1, BK1, 2, third)
-    give_back(ACC0, BK0, 0, 3)
-
-    for c in range(3):
-        out[c] = out[c] + STEP_SIZE * grad[1, c].astype(jnp.float32) * ADJ[...]
-    for n in range(3):
-        wait_sent(n)
-    wait_for(send.at[4], face_tiles, AXES)
+    def gauss():
+        for c in range(3):
+            out[c] = out[c] + STEP_SIZE * grad[1, c].astype(jnp.float32) * ADJ[...]
+        for n in range(3):
+            wait_sent(n)
+        wait_for(send.at[4], face_tiles, AXES)
+
+    give_back(ACC0, BK0, 0, 3, gauss)
 
     def fourth(i, bx, layers):
         for c in range(3):
@@ -494,9 +600,11 @@
 def body(shape, velocity, gradients, shift_x, shift_y, shift_z, fractions):
     TX, TY, TZ = velocity.shape[1:]
     assert TZ == BZ == LANES and TX % VPK == 0 and TX % BX == 0 and TY % BY == 0
+    assert shape["gy"] % 2 == 0 and TX // BX > 1
     assert BX == HX == PK and BY == HY == TILE and XG == 1
     EX, EY = TX + 2 * HX, TY + 2 * HY
     EG = EX // PK
+    NS = 2 if shape["gx"] > 2 else 1
     NB = (TX // BX) * (TY // BY)
     most = EX * EY * (LANES + 2 * HZ) // (TILE * LANES)
 
@@ -515,7 +623,8 @@
             *[pltpu.SMEM(s.shape, s.dtype) for s in (shift_x, shift_y, shift_z, fractions)],
             pltpu.SemaphoreType.DMA((2 * (TX // BX) + 5,)),
             vm(EX + 2 * EG, EY, LANES), vm(EX + 2 * EG, EY, LANES),
-            vm(2, 2, HX + 2 * XG, EY, LANES), vm(EX, EY, LANES),
+            vm(2, NS, HX + 2 * XG, EY, LANES), vm(2, NS, HX + 2 * XG, EY, LANES),
+            vm(2, NS, HX + 2 * XG, HY, LANES), vm(EX, EY, LANES),
             vm(NB, 2, BX + 3, 3 * TILE, LANES), vm(NB, 2, 2 * WX - BX, 5 * TILE, LANES),
             *[vm(EX + 2 * EG, EY, LANES) for _ in range(4)],
             vm(TX, TY, LANES),
@@ -525,7 +634,7 @@
             vm(3, TX // 2, 2 * LH, LANES), vm(3, TX // 2, 2 * LH, LANES),
             vm(3, TX // VPK, TY, LANES), vm(3, TX // VPK, TY, LANES), vm(3, TX // VPK, TY, LANES),
             vm(most, TILE, LANES),
-            pltpu.SemaphoreType.DMA((5,)), pltpu.SemaphoreType.DMA((13,)),
+            pltpu.SemaphoreType.DMA((5,)), pltpu.SemaphoreType.DMA((4 * (1 + 2 * NS) + 1,)),
         ],
         compiler_params=pltpu.CompilerParams(collective_id=0, has_side_effects=True,
                                              vmem_limit_bytes=24 << 20),

time: 26.2 us -> 25.2 us (0.962)
  Pallas kernels: 25.3 us -> 24.3 us
    pallas_call x1, Pallas kernels: 25.3 us -> 24.3 us  [body(): pl.pallas_call(functools.partial(kernel, shape), out_shape=jax.ShapeDtype...]
where the time goes in v2:
time: 25.2 us; the launch traced here: 25.1 us
  Pallas kernels  24.3 us (96%)
  local copies, waits for them, and re-layouts  0.75 us (3%)
    pallas_call x1, Pallas kernels, body(): pl.pallas_call(functools.partial(kernel, shape), out_shape=jax.ShapeDtype...  24.3 us
    unnamed x1, local copies, waits for them, and re-layouts  0.75 us

profile of v2, /device:TPU:0, one launch (start us, length us, event | category | flops | bytes accessed | tf_op | source)
XLA Modules:
  0.0 25.1 jit_solution(15544700409644793743)
XLA Ops:
  0.0 24.3 %shard_map.64 = f32[3,16,16,128]{3,2,1,0:T(8,128)S(1)} custom-call(f32[3,16,16,128]{3,2,1,0:T(8,128)} %vel_in.1, bf16[2,3,16,16,128]{4,3,2,1,0:T(8,128)(2,1)} %grad_in.1, s32[2,2,1,2]{3,2,1,0:T(1,128)} %bitcast.11, s32[2,2,1,2]{3,2,1,0:T(1,128)} %bitcast.12, s32[2,2,1,2]{3,2,1,0:T(1,128)} %bitcast.13, s32[2,2,2,1,3]{4,3,2,1,0:T(1,128)} %bitcast.10), custom_call_target="tpu_custom_call" | custom-call | tf_op jit(solution)/shard_map/pallas_call | solution.py:616
  24.3 0.7 %copy.11 = f32[3,16,16,128]{3,2,1,0:T(8,128)} copy(f32[3,16,16,128]{3,2,1,0:T(8,128)S(1)} %shard_map.64) | data formatting | bytes 786432

commit v3 on v2

--- a/solution.py
+++ b/solution.py
@@ -95,6 +95,12 @@
     def group_of(q):
         return q * up + (EG - 1 - q) * (1 - up)
 
+    def block(j):
+        return (NBY - 1 - j) * even + j * (1 - even)
+
+    def rows_of(t):
+        return pl.ds(multiple(TILE * ((NT + 1 - t) * even + t * (1 - even))), TILE)
+
     loads = []
 
     def load(src, dst):
@@ -142,25 +148,34 @@
     def tiles_of(x, y, z):
         return x * y * z // (TILE * LANES)
 
-    EACH = 1 + 2 * NS
+    EACH = 1 + 3 * NS
     SIDES = [] if shape["gx"] == 1 else [(up, None)] if NS == 1 else [(0, has((-1, 0, 0))), (1, has((1, 0, 0)))]
 
+    def sem(n, kind=None, h=0):
+        return EACH * (n % 2) + (0 if kind is None else 1 + kind * NS + place(h))
+
     def wait_rest(n):
-        wait_for(recv.at[EACH * n], lambda y, z: tiles_of(TX, TY + HY * y, LANES + HZ * z) - tiles_of(TX, TY, LANES),
+        wait_for(recv.at[sem(n)], lambda y, z: tiles_of(TX, TY + HY * y, LANES + HZ * z) - tiles_of(TX, TY, LANES),
                  ("gy", "gz"))
 
     def wait_early(n, h, ok):
-        wait_for(recv.at[EACH * n + 1 + place(h)], lambda z: tiles_of(HX, HY, LANES) + tiles_of(HX, TY, HZ * z), ("gz",), ok)
+        wait_for(recv.at[sem(n, 0, h)], lambda z: tiles_of(HX, HY, LANES + HZ * z), ("gz",), ok)
 
     def wait_late(n, h, ok):
-        wait_for(recv.at[EACH * n + 1 + NS + place(h)], lambda y, z: tiles_of(HX, TY - HY, LANES)
-                 + tiles_of(HX + 2 * XG, HY, LANES) + y * tiles_of(HX, HY, LANES + HZ * z), ("off", "gz"), ok)
+        wait_for(recv.at[sem(n, 1, h)], lambda z: tiles_of(HX, TY - HY, LANES + HZ * z) + tiles_of(HX + 2 * XG, HY, LANES),
+                 ("gz",), ok)
+
+    def wait_off(n, h, ok):
+        wait_for(recv.at[sem(n, 2, h)], lambda y, z: y * tiles_of(HX, HY, LANES + HZ * z), ("off", "gz"), ok)
 
     def wait_back(n, h, ok):
-        wait_for(recv.at[EACH * n + 1 + place(h)], lambda y, z: tiles_of(HX, TY + HY * y, LANES + HZ * z), ("off", "gz"), ok)
+        wait_for(recv.at[sem(n, 0, h)], lambda y, z: tiles_of(HX, TY - HY + HY * y, LANES + HZ * z), ("off", "gz"), ok)
+
+    def wait_last(n, h, ok):
+        wait_for(recv.at[sem(n, 1, h)], lambda z: tiles_of(HX, HY, LANES + HZ * z), ("gz",), ok)
 
     def wait_pair(n, h, ok):
-        wait_for(recv.at[EACH * n + 1 + NS + place(h)], lambda: tiles_of(HX + 2 * XG, HY, LANES), (), ok)
+        wait_for(recv.at[sem(n, 2, h)], lambda: tiles_of(HX + 2 * XG, HY, LANES), (), ok)
 
     def far_of(wait, n):
         if NS == 2:
@@ -227,66 +242,69 @@
         base = {0: 0, -1: EX, 1: EX + EG}[way[2]]
         return ref.at[slice(base + xs.start, base + xs.stop), ys, :]
 
-    def forward_x(E, k, n):
+    def forward_x(E, k, n, part):
         for h, ok in SIDES:
             mine, g, into = pl.ds(HX + h * (TX - HX), HX), XG + h * (G - XG), LX.at[k, place(1 - h)]
-            early, late = EACH * n + 1 + place(1 - h), EACH * n + 1 + NS + place(1 - h)
-            to_device(E.at[mine, A, :], into.at[0:HX, A, :], beside(h), ok, n, early)
-            for z in (-1, 1):
-                to_device(SP.at[k, (z + 1) // 2, g, OY, :], into.at[HX + (1 - z) // 2, OY, :],
-                          beside(h, 0, z), both(ok, has((0, 0, z))), n, early)
-            to_device(E.at[mine, OFF, :], into.at[0:HX, INNER, :], beside(h, -1), both(ok, off), n, late)
-            for z in (-1, 1):
-                to_device(SP.at[k, (z + 1) // 2, g, OFF, :], into.at[HX + (1 - z) // 2, INNER, :],
-                          beside(h, -1, z), both(ok, off, has((0, 0, z))), n, late)
-            to_device(E.at[mine, B, :], into.at[0:HX, B, :], beside(h), ok, n, late)
+
+            def send_rows(rows, where, y, ok, came):
+                to_device(E.at[mine, rows, :], into.at[0:HX, where, :], beside(h, y), ok, n, came)
+                for z in (-1, 1):
+                    to_device(SP.at[k, (z + 1) // 2, g, rows, :], into.at[HX + (1 - z) // 2, where, :],
+                              beside(h, y, z), both(ok, has((0, 0, z))), n, came)
+
+            if part == 0:
+                send_rows(A, A, 0, ok, sem(n, 0, 1 - h))
+            else:
+                send_rows(OFF, INNER, -1, both(ok, off), sem(n, 2, 1 - h))
+                send_rows(B, B, 0, ok, sem(n, 1, 1 - h))
 
     def forward_pair(k, n):
         for h, ok in SIDES:
             wait_early(n, h, ok)
-            to_device(LX.at[k, place(h), :, A, :], LX.at[k, place(h), :, OUTER, :], partner, ok, n,
-                      EACH * n + 1 + NS + place(h))
+            to_device(LX.at[k, place(h), :, A, :], LX.at[k, place(h), :, OUTER, :], partner, ok, n, sem(n, 1, h))
 
     def forward_rest(E, k, n):
         for way in REST:
             xs, ys = region(way, border)
             src = SP.at[k, 0 if way[2] < 0 else 1, xs, ys, :] if way[2] else E.at[xs, ys, :]
-            start(src, rim(E, tuple(-w for w in way)), way, n, EACH * n)
+            start(src, rim(E, tuple(-w for w in way)), way, n, sem(n))
 
     def return_x(k, BK, n, part):
         for h, ok in SIDES:
-            mine, came = HA.at[k, place(h)], EACH * n + 1 + place(1 - h)
+            mine = HA.at[k, place(h)]
             first = (1 - h) * (HX + TX)
             g = (1 - h) * (EG - 1)
 
-            def send_rows(rows, into, y, ok):
+            def send_rows(rows, into, y, ok, came):
                 to_device(mine.at[0:HX, rows, :], BK.at[pl.ds(first, HX), into, :], beside(h, y), ok, n, came)
                 for z in (-1, 1):
                     to_device(mine.at[HX + (z + 1) // 2, rows, :], BK.at[EX + EG * ((1 - z) // 2) + g, into, :],
                               beside(h, y, z), both(ok, has((0, 0, z))), n, came)
 
-            if part == 0:
-                to_device(mine.at[:, INNER, :], RL.at[k, place(h)], partner, ok, n, EACH * n + 1 + NS + place(h))
-                send_rows(OUTER, INNER, -1, both(ok, off))
-                send_rows(B, B, 0, ok)
+            if part == "pair":
+                to_device(mine.at[:, INNER, :], RL.at[k, place(h)], partner, ok, n, sem(n, 2, h))
+            elif part == "off":
+                send_rows(OUTER, INNER, -1, both(ok, off), sem(n, 0, 1 - h))
+            elif part == "own":
+                send_rows(B, B, 0, ok, sem(n, 0, 1 - h))
             else:
                 wait_pair(n, h, ok)
                 for L in range(HX + 2 * XG):
                     HA[k, place(h), L, A, :] = HA[k, place(h), L, A, :] + RL[k, place(h), L]
-                send_rows(A, A, 0, ok)
+                send_rows(A, A, 0, ok, sem(n, 1, 1 - h))
 
     def return_rest(ACC, BK, n):
         for way in REST:
-            start(rim(ACC, way), rim(BK, tuple(-w for w in way)), way, n, EACH * n)
+            start(rim(ACC, way), rim(BK, tuple(-w for w in way)), way, n, sem(n))
 
     REST = [w for w in WAYS if not w[0]]
 
-    def pack_column(E, k, bx):
-        SP[k, 0, XG + bx, OY, :], SP[k, 1, XG + bx, OY, :] = packed(lambda j: E[HX + bx * BX + j, OY, :])
-
-    def unpack(below, above, g):
+    def pack(E, k, bx, rows):
+        SP[k, 0, XG + bx, rows, :], SP[k, 1, XG + bx, rows, :] = packed(lambda j: E[HX + bx * BX + j, rows, :])
+
+    def unpack(below, above, g, rows=slice(None)):
         for j in range(PK):
-            U[PK * g + j] = unpacked(above, below, j)
+            U[PK * g + j, rows, :] = unpacked(above, below, j)
 
     def taps(k, d, bx, by):
         e = frac[k, bx, by, 0, d].astype(jnp.float32) * 0.125
@@ -316,8 +334,7 @@
             res = term if res is None else res + term
         return [res[BY * m:BY * (m + 1)] for m in range(BX)]
 
-    def spread_block(vals, k, i, bx, by):
-        n = i * NBY + by
+    def spread_block(vals, k, n, bx, by):
         c = shz[k, bx, 0, by]
         wx, wy, wz = (taps(k, d, bx, by) for d in range(3))
         flat = jnp.concatenate(vals, axis=0)
@@ -336,62 +353,61 @@
                 XP[n, p, 2 * HX + m, 2 * TILE:2 * TILE + 2 * BY, :] = total_of(
                     wy[v] * YP[n, p, m, TILE - v:TILE - v + 2 * BY, :] for v in range(4))
 
-    def collect(k, q, ACC=None, halo=None):
-        g = group_of(q)
-        found = []
-        for i in range(NBX):
-            if 0 <= q - i <= 2:
-                bx = column(i)
-                offset = BX * ((q - i) * up + (2 - q + i) * (1 - up))
-                for by in range(NBY):
-                    found.append((i * NBY + by, by, (HX + 1) - shx[k, bx, 0, by] + offset,
-                                  (2 * TILE - HY + 1) - shy[k, bx, 0, by]))
-
-        def layer(p, j):
-            tiles = [None] * (EY // TILE)
-            for n, by, x0, y0 in found:
-                rows = XP[n, p, x0 + j, pl.ds(y0, WY), :]
-                for r in range(WY // TILE):
-                    one = rows[r * TILE:(r + 1) * TILE]
-                    old = tiles[by + r]
-                    tiles[by + r] = one if old is None else old + one
-            return jnp.concatenate(tiles, axis=0)
-
-        rims = [layer(1, j) for j in range(PK)]
-        above, below = packed(lambda j: rims[j])
-        for j in range(PK):
-            if halo is not None:
-                HA[k, halo, j] = layer(0, j)
-            else:
-                ACC[PK * g + j] = layer(0, j)
-        if halo is not None:
-            HA[k, halo, HX], HA[k, halo, HX + XG] = below, above
-        else:
-            ACC[EX + EG + g], ACC[EX + g] = above, below
-
-    def received(ACC, BK, i):
+    def collect(k, q, ts, into):
+        for t in ts:
+            found = []
+            for i in range(NBX):
+                for j in range(NBY):
+                    if 0 <= q - i <= 2 and 0 <= t - j <= 2:
+                        bx, by = column(i), block(j)
+                        found.append((i * NBY + j,
+                                      (HX + 1) - shx[k, bx, 0, by] + BX * ((q - i) * up + (2 - q + i) * (1 - up)),
+                                      (2 * TILE - HY + 1) - shy[k, bx, 0, by]
+                                      + TILE * ((2 - t + j) * even + (t - j) * (1 - even))))
+
+            def layer(p, m):
+                return total_of(XP[n, p, x0 + m, pl.ds(y0, TILE), :] for n, x0, y0 in found)
+
+            rims = [layer(1, m) for m in range(PK)]
+            above, below = packed(lambda m: rims[m])
+            into(rows_of(t), [layer(0, m) for m in range(PK)], below, above)
+
+    def collect_own(ACC, k):
+        for q in range(XG, XG + G):
+            g = group_of(q)
+
+            def into(rows, layers, below, above):
+                for m in range(PK):
+                    ACC[PK * g + m, rows, :] = layers[m]
+                ACC[EX + g, rows, :], ACC[EX + EG + g, rows, :] = below, above
+
+            collect(k, q, range(NT + 2), into)
+
+    def collect_halo(k, ts):
+        for q, side in ((EG - 1, place(up)),) + (((0, 1 - up),) if NS == 2 else ()):
+            def into(rows, layers, below, above):
+                for m, one in enumerate(layers + [below, above]):
+                    HA[k, side, m, rows, :] = one
+
+            collect(k, q, ts, into)
+
+    def received(ACC, BK, i, t):
         bx = column(i)
         halos = ([0] if i == 0 and NS == 2 else []) + ([EG - 1] if i == NBX - 1 else [])
         halos = [group_of(q) for q in halos]
 
-        def rows(center, L):
-            tiles = [center[L, HY + TILE * t:HY + TILE * (t + 1), :] for t in range(NT)]
-            tiles[0] = tiles[0] + BK[L, 0:HY, :]
-            tiles[-1] = tiles[-1] + BK[L, HY + TY:, :]
-            return jnp.concatenate(tiles, axis=0)
-
-        rims = []
-        for base in (EX, EX + EG):
-            rims.append(total_of([rows(BK, base + XG + bx)] + [rows(BK, base + g) for g in halos]))
-        first, last = rims
-        res = []
-        for j in range(BX):
-            one = total_of([rows(ACC, HX + bx * BX + j)] + [rows(BK, PK * g + j) for g in halos])
-            res.append(one + jnp.where(edge, unpacked(first, last, j), 0.0))
-        return res
-
-    def blocks(layers, by):
-        return [one[by * BY:(by + 1) * BY] for one in layers]
+        def rows(center, L, pair):
+            terms = [center[L, rows_of(t), :]]
+            if t == 1 and pair:
+                terms.append(BK[L, INNER, :])
+            if t == NT:
+                terms.append(BK[L, OUTER, :])
+            return total_of(terms)
+
+        first, last = (total_of([rows(BK, base + XG + bx, True)] + [rows(BK, base + g, False) for g in halos])
+                       for base in (EX, EX + EG))
+        return [total_of([rows(ACC, HX + bx * BX + m, True)] + [rows(BK, PK * g + m, False) for g in halos])
+                + jnp.where(edge, unpacked(first, last, m), 0.0) for m in range(BX)]
 
     def product(k, bx, j):
         return STEP_SIZE * total_of(grad[k, c, bx * BX + j].astype(jnp.float32) * vel[c, bx * BX + j] for c in range(3))
@@ -411,9 +427,6 @@
             low, high = low + [LX.at[:, 0]], high + [LX.at[:, 1]]
         clear("gx", low + [E.at[x] for E in (E0, E1) for x in sides[0]] + [VE.at[:, 0:LH]],
               high + [E.at[x] for E in (E0, E1) for x in sides[1]] + [VE.at[:, LH + TX:]])
-        for BK in (BK0, BK1):
-            for x in sides[0] + sides[1]:
-                BK[x, INNER, :] = jnp.zeros_like(BK[x, INNER, :])
         ends = slice(0, HY), slice(HY + TY, EY)
         low, high = ([ref.at[:, y] for ref in (E0, E1, BK0, BK1)] + [LX.at[:, :, :, y]] for y in ends)
         clear("gy", low + [YVD], high + [YVU])
@@ -426,7 +439,7 @@
         copies = [((1, 0, 0), vel.at[:, TX - LH:TX], VE.at[:, 0:LH, OY, :]),
                   ((-1, 0, 0), vel.at[:, 0:LH], VE.at[:, LH + TX:2 * LH + TX, OY, :])]
         for way, src, dst in copies:
-            start(src, dst, way, n, EACH * n)
+            start(src, dst, way, n, 2 * EACH)
         VE[:, LH:LH + TX, OY, :] = vel[...]
         for c in range(3):
             for i in range(TX // 2):
@@ -441,14 +454,14 @@
                 SV[c, g] = row
         for way, src, dst in (((0, 1, 0), YSU, YVD), ((0, -1, 0), YSD, YVU),
                               ((0, 0, 1), SV, VRD), ((0, 0, -1), SV, VRU)):
-            start(src, dst, way, n, EACH * n)
+            start(src, dst, way, n, 2 * EACH)
 
     def face_tiles(x, y, z):
         return (x * tiles_of(3 * LH, TY, LANES) + y * tiles_of(3 * TX // 2, 2 * LH, LANES)
                 + z * tiles_of(3 * TX // VPK, TY, LANES))
 
     def regular():
-        wait_for(recv.at[4 * EACH], face_tiles, AXES)
+        wait_for(recv.at[2 * EACH], face_tiles, AXES)
         for c in range(3):
             for i in range(TX // 2):
                 for h in range(2):
@@ -489,10 +502,11 @@
         bx = column(i)
         for j in range(BX):
             E0[HX + bx * BX + j, OY, :] = product(0, bx, j)
-        pack_column(E0, 0, bx)
+        pack(E0, 0, bx, OY)
         if not met and (i == NBX - 1 and NS == 1 or i == 0):
             pl.semaphore_wait(barrier, total)
-            forward_x(E0, 0, 0)
+            forward_x(E0, 0, 0, 0)
+            forward_x(E0, 0, 0, 1)
             met = True
     forward_rest(E0, 0, 0)
 
@@ -507,12 +521,12 @@
     YP[:, :, :, TILE + BY:] = jnp.zeros_like(YP[:, :, :, TILE + BY:])
     XP[...] = jnp.zeros_like(XP)
 
-    def enter(E, k, g, side):
+    def enter(E, k, g, side, rows):
         for j in range(HX):
-            E[PK * g + j] = LX[k, side, j]
-        unpack(LX[k, side, HX], LX[k, side, HX + XG], g)
-
-    def forward(E, n, each):
+            E[PK * g + j, rows, :] = LX[k, side, j, rows, :]
+        unpack(LX[k, side, HX, rows, :], LX[k, side, HX + XG, rows, :], g, rows)
+
+    def forward(E, n, each, after):
         forward_pair(n, n)
         wait_rest(n)
         for i in range(NBX):
@@ -523,61 +537,91 @@
                 g = group_of(0)
                 if NS == 2:
                     far_of(wait_late, n)
-                    enter(E, n, g, 1 - up)
+                    far_of(wait_off, n)
+                    enter(E, n, g, 1 - up, slice(None))
                 else:
                     unpack(E[EX + g], E[EX + EG + g], g)
             if i == NBX - 1:
+                g = group_of(EG - 1)
                 near_of(wait_late, n)
-                enter(E, n, group_of(EG - 1), place(up))
-            each(i, column(i))
-
-    def first(i, bx):
-        for by in range(NBY):
-            res = gather_block(E0, 0, bx, by)
-            for m in range(BX):
-                rows = slice(HY + by * BY, HY + (by + 1) * BY)
-                E1[HX + bx * BX + m, rows, :] = E1[HX + bx * BX + m, rows, :] + res[m]
-        pack_column(E1, 1, bx)
-
-    forward(E0, 0, first)
-    forward_x(E1, 1, 1)
+                enter(E, n, g, place(up), OY)
+                enter(E, n, g, place(up), INNER)
+            for j in range(NBY):
+                if i == NBX - 1 and j == NBY - 1:
+                    near_of(wait_off, n)
+                    enter(E, n, g, place(up), OUTER)
+                each(i * NBY + j, column(i), block(j), rows_of(1 + j))
+                if i == NBX - 1 and j in (0, NBY - 1):
+                    after(j)
+
+    def first(n, bx, by, rows):
+        res = gather_block(E0, 0, bx, by)
+        for m in range(BX):
+            E1[HX + bx * BX + m, rows, :] = E1[HX + bx * BX + m, rows, :] + res[m]
+        pack(E1, 1, bx, rows)
+
+    def first_sent(j):
+        forward_x(E1, 1, 1, min(j, 1))
+
+    forward(E0, 0, first, first_sent)
     forward_rest(E1, 1, 1)
 
-    def second(i, bx):
-        for by in range(NBY):
-            spread_block(gather_block(E1, 1, bx, by), 1, i, bx, by)
-
-    forward(E1, 1, second)
+    def second(n, bx, by, rows):
+        spread_block(gather_block(E1, 1, bx, by), 1, n, bx, by)
+
+    def second_sent(j):
+        if j == 0:
+            collect_halo(1, [0])
+            return_x(1, BK1, 2, "pair")
+        else:
+            collect_halo(1, [NT + 1])
+            return_x(1, BK1, 2, "off")
+
+    forward(E1, 1, second, second_sent)
 
     def give_back(ACC, BK, k, n, meanwhile):
-        collect(k, EG - 1, halo=place(up))
-        if NS == 2:
-            collect(k, 0, halo=1 - up)
-        return_x(k, BK, n, 0)
-        for q in range(XG, XG + G):
-            collect(k, q, ACC)
+        collect_halo(k, range(1, NT + 1))
+        return_x(k, BK, n, "own")
+        collect_own(ACC, k)
         return_rest(ACC, BK, n)
         meanwhile()
-        return_x(k, BK, n, 1)
-
-    def backward(ACC, BK, n, each):
+        return_x(k, BK, n, "sum")
+
+    def backward(ACC, BK, n, each, after):
         wait_rest(n)
         for i in range(NBX):
             if i == 0:
                 far_of(wait_back, n)
+                far_of(wait_last, n)
             if i == NBX - 1:
                 near_of(wait_back, n)
-            each(i, column(i), received(ACC, BK, i))
+            for j in reversed(range(NBY)):
+                if i == NBX - 1 and j == 0:
+                    near_of(wait_last, n)
+                each(i * NBY + j, column(i), block(j), 1 + j, received(ACC, BK, i, 1 + j))
+                if i == NBX - 1 and j in (0, NBY - 1):
+                    after(j)
 
     give_back(ACC1, BK1, 1, 2, regular)
 
-    def third(i, bx, layers):
-        for j in range(BX):
-            ADJ[bx * BX + j] = layers[j]
-        for by in range(NBY):
-            spread_block(blocks(layers, by), 0, i, bx, by)
-
-    backward(ACC1, BK1, 2, third)
+    def own_rows(t):
+        return pl.ds(multiple(TILE * ((NT - t) * even + (t - 1) * (1 - even))), TILE)
+
+    def third(n, bx, by, t, layers):
+        for m in range(BX):
+            ADJ[bx * BX + m, own_rows(t), :] = layers[m]
+        spread_block(layers, 0, n, bx, by)
+
+    def third_sent(j):
+        if j == 0:
+            collect_halo(0, [0])
+            return_x(0, BK0, 3, "pair")
+        else:
+            collect_halo(0, [NT + 1])
+            return_x(0, BK0, 3, "off")
+
+    backward(ACC1, BK1, 2, third, third_sent)
+
     def gauss():
         for c in range(3):
             out[c] = out[c] + STEP_SIZE * grad[1, c].astype(jnp.float32) * ADJ[...]
@@ -587,20 +631,23 @@
 
     give_back(ACC0, BK0, 0, 3, gauss)
 
-    def fourth(i, bx, layers):
-        for c in range(3):
-            for j in range(BX):
-                x = bx * BX + j
-                out[c, x] = out[c, x] + STEP_SIZE * grad[0, c, x].astype(jnp.float32) * layers[j]
-
-    backward(ACC0, BK0, 3, fourth)
+    def fourth(n, bx, by, t, layers):
+        for m in range(BX):
+            ADJ[bx * BX + m, own_rows(t), :] = layers[m]
+        if t == 1:
+            for c in range(3):
+                for m in range(BX):
+                    x = bx * BX + m
+                    out[c, x] = out[c, x] + STEP_SIZE * grad[0, c, x].astype(jnp.float32) * ADJ[x]
+
+    backward(ACC0, BK0, 3, fourth, lambda j: None)
     wait_sent(3)
 
 
 def body(shape, velocity, gradients, shift_x, shift_y, shift_z, fractions):
     TX, TY, TZ = velocity.shape[1:]
     assert TZ == BZ == LANES and TX % VPK == 0 and TX % BX == 0 and TY % BY == 0
-    assert shape["gy"] % 2 == 0 and TX // BX > 1
+    assert shape["gy"] % 2 == 0 and TX // BX > 1 and TY // BY > 1
     assert BX == HX == PK and BY == HY == TILE and XG == 1
     EX, EY = TX + 2 * HX, TY + 2 * HY
     EG = EX // PK
@@ -634,7 +681,7 @@
             vm(3, TX // 2, 2 * LH, LANES), vm(3, TX // 2, 2 * LH, LANES),
             vm(3, TX // VPK, TY, LANES), vm(3, TX // VPK, TY, LANES), vm(3, TX // VPK, TY, LANES),
             vm(most, TILE, LANES),
-            pltpu.SemaphoreType.DMA((5,)), pltpu.SemaphoreType.DMA((4 * (1 + 2 * NS) + 1,)),
+            pltpu.SemaphoreType.DMA((5,)), pltpu.SemaphoreType.DMA((2 * (1 + 3 * NS) + 1,)),
         ],
         compiler_params=pltpu.CompilerParams(collective_id=0, has_side_effects=True,
                                              vmem_limit_bytes=24 << 20),

time: 25.2 us -> 25.9 us (1.028)
  Pallas kernels: 24.3 us -> 25 us
    pallas_call x1, Pallas kernels: 24.3 us -> 25 us  [body(): pl.pallas_call(functools.partial(kernel, shape), out_shape=jax.ShapeDtype...]
where the time goes in v3:
time: 25.9 us; the launch traced here: 25.7 us
  Pallas kernels  25 us (97%)
  local copies, waits for them, and re-layouts  0.75 us (3%)
    pallas_call x1, Pallas kernels, body(): pl.pallas_call(functools.partial(kernel, shape), out_shape=jax.ShapeDtype...  25 us
    unnamed x1, local copies, waits for them, and re-layouts  0.75 us

profile of v3, /device:TPU:0, one launch (start us, length us, event | category | flops | bytes accessed | tf_op | source)
XLA Modules:
  0.0 25.7 jit_solution(6237117074570386601)
XLA Ops:
  0.0 25.0 %shard_map.64 = f32[3,16,16,128]{3,2,1,0:T(8,128)S(1)} custom-call(f32[3,16,16,128]{3,2,1,0:T(8,128)} %vel_in.1, bf16[2,3,16,16,128]{4,3,2,1,0:T(8,128)(2,1)} %grad_in.1, s32[2,2,1,2]{3,2,1,0:T(1,128)} %bitcast.11, s32[2,2,1,2]{3,2,1,0:T(1,128)} %bitcast.12, s32[2,2,1,2]{3,2,1,0:T(1,128)} %bitcast.13, s32[2,2,2,1,3]{4,3,2,1,0:T(1,128)} %bitcast.10), custom_call_target="tpu_custom_call" | custom-call | tf_op jit(solution)/shard_map/pallas_call | solution.py:663
  25.0 0.7 %copy.11 = f32[3,16,16,128]{3,2,1,0:T(8,128)} copy(f32[3,16,16,128]{3,2,1,0:T(8,128)S(1)} %shard_map.64) | data formatting | bytes 786432

commit v4 on v2

--- a/solution.py
+++ b/solution.py
@@ -95,20 +95,16 @@
     def group_of(q):
         return q * up + (EG - 1 - q) * (1 - up)
 
-    loads = []
-
-    def load(src, dst):
-        loads.append(pltpu.make_async_copy(src, dst, arrive.at[len(loads)]))
-        loads[-1].start()
-        return loads[-1]
-
     def part(ref, i):
         return ref.at[:, pl.ds(column(i) * BX, BX)]
 
-    sources = [(load(part(vel_in, i), part(vel, i)), load(part(grad_in.at[0], i), part(grad.at[0], i)))
-               for i in reversed(range(NBX))]
-    later = [load(a, b) for a, b in ((shx_in, shx), (shy_in, shy), (shz_in, shz), (frac_in, frac),
-                                     (grad_in.at[1], grad.at[1]))]
+    for i in reversed(range(NBX)):
+        for src, dst in ((vel_in, vel), (grad_in.at[0], grad.at[0])):
+            pltpu.make_async_copy(part(src, i), part(dst, i), arrive.at[i]).start()
+    later = [pltpu.make_async_copy(a, b, arrive.at[NBX + m]) for m, (a, b) in enumerate((
+        (shx_in, shx), (shy_in, shy), (shz_in, shz), (frac_in, frac), (grad_in.at[1], grad.at[1])))]
+    for copy in later:
+        copy.start()
 
     barrier = pltpu.get_barrier_semaphore()
     total = jnp.int32(0)
@@ -145,22 +141,25 @@
     EACH = 1 + 2 * NS
     SIDES = [] if shape["gx"] == 1 else [(up, None)] if NS == 1 else [(0, has((-1, 0, 0))), (1, has((1, 0, 0)))]
 
+    def sem(n, kind=None, h=0):
+        return EACH * (n % 2) + (0 if kind is None else 1 + kind * NS + place(h))
+
     def wait_rest(n):
-        wait_for(recv.at[EACH * n], lambda y, z: tiles_of(TX, TY + HY * y, LANES + HZ * z) - tiles_of(TX, TY, LANES),
+        wait_for(recv.at[sem(n)], lambda y, z: tiles_of(TX, TY + HY * y, LANES + HZ * z) - tiles_of(TX, TY, LANES),
                  ("gy", "gz"))
 
     def wait_early(n, h, ok):
-        wait_for(recv.at[EACH * n + 1 + place(h)], lambda z: tiles_of(HX, HY, LANES) + tiles_of(HX, TY, HZ * z), ("gz",), ok)
+        wait_for(recv.at[sem(n, 0, h)], lambda z: tiles_of(HX, HY, LANES + HZ * z), ("gz",), ok)
 
     def wait_late(n, h, ok):
-        wait_for(recv.at[EACH * n + 1 + NS + place(h)], lambda y, z: tiles_of(HX, TY - HY, LANES)
-                 + tiles_of(HX + 2 * XG, HY, LANES) + y * tiles_of(HX, HY, LANES + HZ * z), ("off", "gz"), ok)
+        wait_for(recv.at[sem(n, 1, h)], lambda y, z: tiles_of(HX, TY - HY + HY * y, LANES + HZ * z)
+                 + tiles_of(HX + 2 * XG, HY, LANES), ("off", "gz"), ok)
 
     def wait_back(n, h, ok):
-        wait_for(recv.at[EACH * n + 1 + place(h)], lambda y, z: tiles_of(HX, TY + HY * y, LANES + HZ * z), ("off", "gz"), ok)
+        wait_for(recv.at[sem(n, 0, h)], lambda y, z: tiles_of(HX, TY + HY * y, LANES + HZ * z), ("off", "gz"), ok)
 
     def wait_pair(n, h, ok):
-        wait_for(recv.at[EACH * n + 1 + NS + place(h)], lambda: tiles_of(HX + 2 * XG, HY, LANES), (), ok)
+        wait_for(recv.at[sem(n, 1, h)], lambda: tiles_of(HX + 2 * XG, HY, LANES), (), ok)
 
     def far_of(wait, n):
         if NS == 2:
@@ -170,17 +169,20 @@
         for h, ok in SIDES:
             wait(n, h, jnp.logical_and(ok, up == 1) if NS == 2 and h else ok)
 
-    def wait_sent(n):
-        wait_for(send.at[n], lambda x, y, z: tiles_of(TX, TY + HY * (1 + y), LANES + HZ * z) - tiles_of(TX, TY, LANES)
-                 + x * (tiles_of(HX, TY + HY * y, LANES + HZ * z) + tiles_of(HX + 2 * XG, HY, LANES)),
-                 ("gx", "off", "gz"))
-
-    def start(src, dst, way, sent, came):
-        to_device(src, dst, device(way), has(way), sent, came)
-
-    def to_device(src, dst, where, ok, sent, came):
+    def wait_sent():
+        def tiles(x, y, z):
+            one = (tiles_of(TX, TY + HY * (1 + y), LANES + HZ * z) - tiles_of(TX, TY, LANES)
+                   + x * (tiles_of(HX, TY + HY * y, LANES + HZ * z) + tiles_of(HX + 2 * XG, HY, LANES)))
+            return 2 * STEPS * one + face_tiles(x, 1 + y, z)
+
+        wait_for(send.at[0], tiles, ("gx", "off", "gz"))
+
+    def start(src, dst, way, came):
+        to_device(src, dst, device(way), has(way), came)
+
+    def to_device(src, dst, where, ok, came):
         desc = pltpu.make_async_remote_copy(
-            src_ref=src, dst_ref=dst, send_sem=send.at[sent], recv_sem=recv.at[came],
+            src_ref=src, dst_ref=dst, send_sem=send.at[0], recv_sem=recv.at[came],
             device_id=where, device_id_type=MESH)
         if ok is None:
             desc.start()
@@ -230,43 +232,46 @@
     def forward_x(E, k, n):
         for h, ok in SIDES:
             mine, g, into = pl.ds(HX + h * (TX - HX), HX), XG + h * (G - XG), LX.at[k, place(1 - h)]
-            early, late = EACH * n + 1 + place(1 - h), EACH * n + 1 + NS + place(1 - h)
-            to_device(E.at[mine, A, :], into.at[0:HX, A, :], beside(h), ok, n, early)
-            for z in (-1, 1):
-                to_device(SP.at[k, (z + 1) // 2, g, OY, :], into.at[HX + (1 - z) // 2, OY, :],
-                          beside(h, 0, z), both(ok, has((0, 0, z))), n, early)
-            to_device(E.at[mine, OFF, :], into.at[0:HX, INNER, :], beside(h, -1), both(ok, off), n, late)
-            for z in (-1, 1):
-                to_device(SP.at[k, (z + 1) // 2, g, OFF, :], into.at[HX + (1 - z) // 2, INNER, :],
-                          beside(h, -1, z), both(ok, off, has((0, 0, z))), n, late)
-            to_device(E.at[mine, B, :], into.at[0:HX, B, :], beside(h), ok, n, late)
+
+            def send_rows(rows, where, y, ok, came):
+                to_device(E.at[mine, rows, :], into.at[0:HX, where, :], beside(h, y), ok, came)
+                for z in (-1, 1):
+                    to_device(SP.at[k, (z + 1) // 2, g, rows, :], into.at[HX + (1 - z) // 2, where, :],
+                              beside(h, y, z), both(ok, has((0, 0, z))), came)
+
+            send_rows(A, A, 0, ok, sem(n, 0, 1 - h))
+            send_rows(OFF, INNER, -1, both(ok, off), sem(n, 1, 1 - h))
+            send_rows(B, B, 0, ok, sem(n, 1, 1 - h))
 
     def forward_pair(k, n):
         for h, ok in SIDES:
             wait_early(n, h, ok)
-            to_device(LX.at[k, place(h), :, A, :], LX.at[k, place(h), :, OUTER, :], partner, ok, n,
-                      EACH * n + 1 + NS + place(h))
-
-    def forward_rest(E, k, n):
+            to_device(LX.at[k, place(h), :, A, :], LX.at[k, place(h), :, OUTER, :], partner, ok, sem(n, 1, h))
+
+    def forward_rest(E, k, n, bx):
         for way in REST:
-            xs, ys = region(way, border)
-            src = SP.at[k, 0 if way[2] < 0 else 1, xs, ys, :] if way[2] else E.at[xs, ys, :]
-            start(src, rim(E, tuple(-w for w in way)), way, n, EACH * n)
+            ys, into = region(way, border)[1], region(tuple(-w for w in way), piece)[1]
+            base = {0: HX, -1: EX + EG, 1: EX}[way[2]]
+            if way[2]:
+                src, dst = SP.at[k, (way[2] + 1) // 2, XG + bx, ys, :], E.at[base + XG + bx, into, :]
+            else:
+                src, dst = (E.at[pl.ds(HX + bx * BX, BX), rows, :] for rows in (ys, into))
+            start(src, dst, way, sem(n))
 
     def return_x(k, BK, n, part):
         for h, ok in SIDES:
-            mine, came = HA.at[k, place(h)], EACH * n + 1 + place(1 - h)
+            mine, came = HA.at[k, place(h)], sem(n, 0, 1 - h)
             first = (1 - h) * (HX + TX)
             g = (1 - h) * (EG - 1)
 
             def send_rows(rows, into, y, ok):
-                to_device(mine.at[0:HX, rows, :], BK.at[pl.ds(first, HX), into, :], beside(h, y), ok, n, came)
+                to_device(mine.at[0:HX, rows, :], BK.at[pl.ds(first, HX), into, :], beside(h, y), ok, came)
                 for z in (-1, 1):
                     to_device(mine.at[HX + (z + 1) // 2, rows, :], BK.at[EX + EG * ((1 - z) // 2) + g, into, :],
-                              beside(h, y, z), both(ok, has((0, 0, z))), n, came)
+                              beside(h, y, z), both(ok, has((0, 0, z))), came)
 
             if part == 0:
-                to_device(mine.at[:, INNER, :], RL.at[k, place(h)], partner, ok, n, EACH * n + 1 + NS + place(h))
+                to_device(mine.at[:, INNER, :], RL.at[k, place(h)], partner, ok, sem(n, 1, h))
                 send_rows(OUTER, INNER, -1, both(ok, off))
                 send_rows(B, B, 0, ok)
             else:
@@ -277,7 +282,7 @@
 
     def return_rest(ACC, BK, n):
         for way in REST:
-            start(rim(ACC, way), rim(BK, tuple(-w for w in way)), way, n, EACH * n)
+            start(rim(ACC, way), rim(BK, tuple(-w for w in way)), way, sem(n))
 
     REST = [w for w in WAYS if not w[0]]
 
@@ -422,11 +427,10 @@
               high + [LX.at[:, :, HX + XG, y] for y in (OY, OUTER)] + [VRU])
 
     def send_faces():
-        n = 4
         copies = [((1, 0, 0), vel.at[:, TX - LH:TX], VE.at[:, 0:LH, OY, :]),
                   ((-1, 0, 0), vel.at[:, 0:LH], VE.at[:, LH + TX:2 * LH + TX, OY, :])]
         for way, src, dst in copies:
-            start(src, dst, way, n, EACH * n)
+            start(src, dst, way, 2 * EACH)
         VE[:, LH:LH + TX, OY, :] = vel[...]
         for c in range(3):
             for i in range(TX // 2):
@@ -441,14 +445,14 @@
                 SV[c, g] = row
         for way, src, dst in (((0, 1, 0), YSU, YVD), ((0, -1, 0), YSD, YVU),
                               ((0, 0, 1), SV, VRD), ((0, 0, -1), SV, VRU)):
-            start(src, dst, way, n, EACH * n)
+            start(src, dst, way, 2 * EACH)
 
     def face_tiles(x, y, z):
         return (x * tiles_of(3 * LH, TY, LANES) + y * tiles_of(3 * TX // 2, 2 * LH, LANES)
                 + z * tiles_of(3 * TX // VPK, TY, LANES))
 
     def regular():
-        wait_for(recv.at[4 * EACH], face_tiles, AXES)
+        wait_for(recv.at[2 * EACH], face_tiles, AXES)
         for c in range(3):
             for i in range(TX // 2):
                 for h in range(2):
@@ -484,8 +488,7 @@
 
     met = False
     for i in reversed(range(NBX)):
-        for copy in sources[NBX - 1 - i]:
-            copy.wait()
+        wait_for(arrive.at[i], lambda: tiles_of(3 * BX, TY, LANES) * 3 // 2, ())
         bx = column(i)
         for j in range(BX):
             E0[HX + bx * BX + j, OY, :] = product(0, bx, j)
@@ -494,7 +497,8 @@
             pl.semaphore_wait(barrier, total)
             forward_x(E0, 0, 0)
             met = True
-    forward_rest(E0, 0, 0)
+    for i in range(NBX):
+        forward_rest(E0, 0, 0, column(i))
 
     clear_missing()
     send_faces()
@@ -538,10 +542,11 @@
                 rows = slice(HY + by * BY, HY + (by + 1) * BY)
                 E1[HX + bx * BX + m, rows, :] = E1[HX + bx * BX + m, rows, :] + res[m]
         pack_column(E1, 1, bx)
+        if i == NBX - 1:
+            forward_x(E1, 1, 1)
+        forward_rest(E1, 1, 1, bx)
 
     forward(E0, 0, first)
-    forward_x(E1, 1, 1)
-    forward_rest(E1, 1, 1)
 
     def second(i, bx):
         for by in range(NBY):
@@ -581,9 +586,6 @@
     def gauss():
         for c in range(3):
             out[c] = out[c] + STEP_SIZE * grad[1, c].astype(jnp.float32) * ADJ[...]
-        for n in range(3):
-            wait_sent(n)
-        wait_for(send.at[4], face_tiles, AXES)
 
     give_back(ACC0, BK0, 0, 3, gauss)
 
@@ -594,7 +596,7 @@
                 out[c, x] = out[c, x] + STEP_SIZE * grad[0, c, x].astype(jnp.float32) * layers[j]
 
     backward(ACC0, BK0, 3, fourth)
-    wait_sent(3)
+    wait_sent()
 
 
 def body(shape, velocity, gradients, shift_x, shift_y, shift_z, fractions):
@@ -606,7 +608,7 @@
     EG = EX // PK
     NS = 2 if shape["gx"] > 2 else 1
     NB = (TX // BX) * (TY // BY)
-    most = EX * EY * (LANES + 2 * HZ) // (TILE * LANES)
+    most = (2 * STEPS + 1) * EX * EY * (LANES + 2 * HZ) // (TILE * LANES)
 
     vm = lambda *s: pltpu.VMEM(s, jnp.float32)
     vmem = pl.BlockSpec(memory_space=pltpu.VMEM)
@@ -621,7 +623,7 @@
         scratch_shapes=[
             pltpu.VMEM(velocity.shape, velocity.dtype), pltpu.VMEM(gradients.shape, gradients.dtype),
             *[pltpu.SMEM(s.shape, s.dtype) for s in (shift_x, shift_y, shift_z, fractions)],
-            pltpu.SemaphoreType.DMA((2 * (TX // BX) + 5,)),
+            pltpu.SemaphoreType.DMA((TX // BX + 5,)),
             vm(EX + 2 * EG, EY, LANES), vm(EX + 2 * EG, EY, LANES),
             vm(2, NS, HX + 2 * XG, EY, LANES), vm(2, NS, HX + 2 * XG, EY, LANES),
             vm(2, NS, HX + 2 * XG, HY, LANES), vm(EX, EY, LANES),
@@ -634,7 +636,7 @@
             vm(3, TX // 2, 2 * LH, LANES), vm(3, TX // 2, 2 * LH, LANES),
             vm(3, TX // VPK, TY, LANES), vm(3, TX // VPK, TY, LANES), vm(3, TX // VPK, TY, LANES),
             vm(most, TILE, LANES),
-            pltpu.SemaphoreType.DMA((5,)), pltpu.SemaphoreType.DMA((4 * (1 + 2 * NS) + 1,)),
+            pltpu.SemaphoreType.DMA((1,)), pltpu.SemaphoreType.DMA((2 * (1 + 2 * NS) + 1,)),
         ],
         compiler_params=pltpu.CompilerParams(collective_id=0, has_side_effects=True,
                                              vmem_limit_bytes=24 << 20),

time: 25.2 us -> 24.8 us (0.984)
  Pallas kernels: 24.3 us -> 23.9 us
    pallas_call x1, Pallas kernels: 24.3 us -> 23.9 us  [body(): pl.pallas_call(functools.partial(kernel, shape), out_shape=jax.ShapeDtype...]
where the time goes in v4:
time: 24.8 us; the launch traced here: 24.7 us
  Pallas kernels  23.9 us (96%)
  local copies, waits for them, and re-layouts  0.75 us (3%)
    pallas_call x1, Pallas kernels, body(): pl.pallas_call(functools.partial(kernel, shape), out_shape=jax.ShapeDtype...  23.9 us
    unnamed x1, local copies, waits for them, and re-layouts  0.75 us

profile of v4, /device:TPU:0, one launch (start us, length us, event | category | flops | bytes accessed | tf_op | source)
XLA Modules:
  0.0 24.7 jit_solution(11489171991941475965)
XLA Ops:
  0.0 23.9 %shard_map.64 = f32[3,16,16,128]{3,2,1,0:T(8,128)S(1)} custom-call(f32[3,16,16,128]{3,2,1,0:T(8,128)} %vel_in.1, bf16[2,3,16,16,128]{4,3,2,1,0:T(8,128)(2,1)} %grad_in.1, s32[2,2,1,2]{3,2,1,0:T(1,128)} %bitcast.11, s32[2,2,1,2]{3,2,1,0:T(1,128)} %bitcast.12, s32[2,2,1,2]{3,2,1,0:T(1,128)} %bitcast.13, s32[2,2,2,1,3]{4,3,2,1,0:T(1,128)} %bitcast.10), custom_call_target="tpu_custom_call" | custom-call | tf_op jit(solution)/shard_map/pallas_call | solution.py:618
  23.9 0.7 %copy.11 = f32[3,16,16,128]{3,2,1,0:T(8,128)} copy(f32[3,16,16,128]{3,2,1,0:T(8,128)S(1)} %shard_map.64) | data formatting | bytes 786432

commit v5 on v4

--- a/solution.py
+++ b/solution.py
@@ -77,6 +77,9 @@
     even = 1 - lax.rem(at["gy"], 2)
     off = jnp.where(even == 1, at["gy"] > 0, at["gy"] < shape["gy"] - 1)
 
+    odd = even == 0
+    SEAM = pl.ds(0, 2 * HY), pl.ds(TY, 2 * HY)
+
     def place(h):
         return h if NS == 2 else 0
 
@@ -115,6 +118,8 @@
         total = total + has(way).astype(jnp.int32)
 
     def counts(a):
+        if a == "even":
+            return [(v, even == v) for v in range(2)]
         if a == "off":
             return [(v, off if v else jnp.logical_not(off)) for v in range(2)] if shape["gy"] > 2 else [(0, None)]
         n = (at[a] > 0).astype(jnp.int32) + (at[a] < shape[a] - 1).astype(jnp.int32)
@@ -149,17 +154,17 @@
                  ("gy", "gz"))
 
     def wait_early(n, h, ok):
-        wait_for(recv.at[sem(n, 0, h)], lambda z: tiles_of(HX, HY, LANES + HZ * z), ("gz",), ok)
+        wait_for(recv.at[sem(n, 0, h)], lambda z: 2 * tiles_of(HX, HY, LANES + HZ * z), ("gz",), both(ok, odd))
 
     def wait_late(n, h, ok):
-        wait_for(recv.at[sem(n, 1, h)], lambda y, z: tiles_of(HX, TY - HY + HY * y, LANES + HZ * z)
-                 + tiles_of(HX + 2 * XG, HY, LANES), ("off", "gz"), ok)
+        wait_for(recv.at[sem(n, 1, h)], lambda e, y, z: tiles_of(HX, TY - HY + HY * y, LANES + HZ * z)
+                 + e * tiles_of(HX + 2 * XG, 2 * HY, LANES), ("even", "off", "gz"), ok)
 
     def wait_back(n, h, ok):
         wait_for(recv.at[sem(n, 0, h)], lambda y, z: tiles_of(HX, TY + HY * y, LANES + HZ * z), ("off", "gz"), ok)
 
     def wait_pair(n, h, ok):
-        wait_for(recv.at[sem(n, 1, h)], lambda: tiles_of(HX + 2 * XG, HY, LANES), (), ok)
+        wait_for(recv.at[sem(n, 1, h)], lambda: tiles_of(HX + 2 * XG, 2 * HY, LANES), (), both(ok, odd))
 
     def far_of(wait, n):
         if NS == 2:
@@ -170,12 +175,13 @@
             wait(n, h, jnp.logical_and(ok, up == 1) if NS == 2 and h else ok)
 
     def wait_sent():
-        def tiles(x, y, z):
-            one = (tiles_of(TX, TY + HY * (1 + y), LANES + HZ * z) - tiles_of(TX, TY, LANES)
-                   + x * (tiles_of(HX, TY + HY * y, LANES + HZ * z) + tiles_of(HX + 2 * XG, HY, LANES)))
-            return 2 * STEPS * one + face_tiles(x, 1 + y, z)
-
-        wait_for(send.at[0], tiles, ("gx", "off", "gz"))
+        def tiles(x, e, y, z):
+            seam = tiles_of(HX + 2 * XG, 2 * HY, LANES)
+            along = seam + tiles_of(HX, 2 * (TY + HY * y) + (-HY if e else HY), LANES + HZ * z)
+            one = tiles_of(TX, TY + HY * (1 + y), LANES + HZ * z) - tiles_of(TX, TY, LANES)
+            return STEPS * (2 * one + x * along) + face_tiles(x, 1 + y, z)
+
+        wait_for(send.at[0], tiles, ("gx", "even", "off", "gz"))
 
     def start(src, dst, way, came):
         to_device(src, dst, device(way), has(way), came)
@@ -195,7 +201,9 @@
 
     def beside(h, y=0, z=0):
         where = {"gx": at["gx"] + 2 * h - 1}
-        if y:
+        if y is even:
+            where["gy"] = at["gy"] + even
+        elif y:
             where["gy"] = at["gy"] + (1 - 2 * even if y < 0 else 2 * even - 1)
         if z:
             where["gz"] = at["gz"] + z
@@ -239,14 +247,15 @@
                     to_device(SP.at[k, (z + 1) // 2, g, rows, :], into.at[HX + (1 - z) // 2, where, :],
                               beside(h, y, z), both(ok, has((0, 0, z))), came)
 
-            send_rows(A, A, 0, ok, sem(n, 0, 1 - h))
+            send_rows(A, pl.ds(multiple(HY * (1 - even)), HY), even, ok, sem(n, 0, 1 - h))
             send_rows(OFF, INNER, -1, both(ok, off), sem(n, 1, 1 - h))
             send_rows(B, B, 0, ok, sem(n, 1, 1 - h))
 
     def forward_pair(k, n):
         for h, ok in SIDES:
             wait_early(n, h, ok)
-            to_device(LX.at[k, place(h), :, A, :], LX.at[k, place(h), :, OUTER, :], partner, ok, sem(n, 1, h))
+            to_device(LX.at[k, place(h), :, SEAM[0], :], LX.at[k, place(h), :, SEAM[1], :], partner, both(ok, odd),
+                      sem(n, 1, h))
 
     def forward_rest(E, k, n, bx):
         for way in REST:
@@ -271,14 +280,19 @@
                               beside(h, y, z), both(ok, has((0, 0, z))), came)
 
             if part == 0:
-                to_device(mine.at[:, INNER, :], RL.at[k, place(h)], partner, ok, sem(n, 1, h))
+                to_device(mine.at[:, SEAM[1], :], RL.at[k, place(h)], partner, both(ok, even == 1), sem(n, 1, h))
                 send_rows(OUTER, INNER, -1, both(ok, off))
                 send_rows(B, B, 0, ok)
             else:
                 wait_pair(n, h, ok)
-                for L in range(HX + 2 * XG):
-                    HA[k, place(h), L, A, :] = HA[k, place(h), L, A, :] + RL[k, place(h), L]
-                send_rows(A, A, 0, ok)
+
+                @pl.when(odd)
+                def _(h=h):
+                    for L in range(HX + 2 * XG):
+                        HA[k, place(h), L, SEAM[0], :] = HA[k, place(h), L, SEAM[0], :] + RL[k, place(h), L]
+
+                send_rows(pl.ds(0, HY), pl.ds(TY, HY), 1, both(ok, odd))
+                send_rows(pl.ds(HY, HY), pl.ds(HY, HY), 0, both(ok, odd))
 
     def return_rest(ACC, BK, n):
         for way in REST:
@@ -423,8 +437,11 @@
         low, high = ([ref.at[:, y] for ref in (E0, E1, BK0, BK1)] + [LX.at[:, :, :, y]] for y in ends)
         clear("gy", low + [YVD], high + [YVU])
         low, high = ([ref.at[x] for ref in (E0, E1, BK0, BK1)] for x in (slice(EX, EX + EG), slice(EX + EG, EX + 2 * EG)))
-        clear("gz", low + [LX.at[:, :, HX, y] for y in (OY, OUTER)] + [VRD],
-              high + [LX.at[:, :, HX + XG, y] for y in (OY, OUTER)] + [VRU])
+        clear("gz", low + [LX.at[:, :, HX, 0:TY], VRD], high + [LX.at[:, :, HX + XG, 0:TY], VRU])
+        for end, L in ((0, HX), (shape["gz"] - 1, HX + XG)):
+            @pl.when(jnp.logical_and(at["gz"] == end, odd))
+            def _(L=L):
+                LX[:, :, L, TY:, :] = jnp.zeros_like(LX[:, :, L, TY:, :])
 
     def send_faces():
         copies = [((1, 0, 0), vel.at[:, TX - LH:TX], VE.at[:, 0:LH, OY, :]),
@@ -626,7 +643,7 @@
             pltpu.SemaphoreType.DMA((TX // BX + 5,)),
             vm(EX + 2 * EG, EY, LANES), vm(EX + 2 * EG, EY, LANES),
             vm(2, NS, HX + 2 * XG, EY, LANES), vm(2, NS, HX + 2 * XG, EY, LANES),
-            vm(2, NS, HX + 2 * XG, HY, LANES), vm(EX, EY, LANES),
+            vm(2, NS, HX + 2 * XG, 2 * HY, LANES), vm(EX, EY, LANES),
             vm(NB, 2, BX + 3, 3 * TILE, LANES), vm(NB, 2, 2 * WX - BX, 5 * TILE, LANES),
             *[vm(EX + 2 * EG, EY, LANES) for _ in range(4)],
             vm(TX, TY, LANES),

time: 24.8 us -> 24.2 us (0.976)
  Pallas kernels: 23.9 us -> 23.4 us
    pallas_call x1, Pallas kernels: 23.9 us -> 23.4 us  [body(): pl.pallas_call(functools.partial(kernel, shape), out_shape=jax.ShapeDtype...]
where the time goes in v5:
time: 24.2 us; the launch traced here: 24.1 us
  Pallas kernels  23.4 us (97%)
  local copies, waits for them, and re-layouts  0.75 us (3%)
    pallas_call x1, Pallas kernels, body(): pl.pallas_call(functools.partial(kernel, shape), out_shape=jax.ShapeDtype...  23.4 us
    unnamed x1, local copies, waits for them, and re-layouts  0.75 us

profile of v5, /device:TPU:0, one launch (start us, length us, event | category | flops | bytes accessed | tf_op | source)
XLA Modules:
  0.0 24.1 jit_solution(9813655184147392480)
XLA Ops:
  0.0 23.4 %shard_map.64 = f32[3,16,16,128]{3,2,1,0:T(8,128)S(1)} custom-call(f32[3,16,16,128]{3,2,1,0:T(8,128)} %vel_in.1, bf16[2,3,16,16,128]{4,3,2,1,0:T(8,128)(2,1)} %grad_in.1, s32[2,2,1,2]{3,2,1,0:T(1,128)} %bitcast.11, s32[2,2,1,2]{3,2,1,0:T(1,128)} %bitcast.12, s32[2,2,1,2]{3,2,1,0:T(1,128)} %bitcast.13, s32[2,2,2,1,3]{4,3,2,1,0:T(1,128)} %bitcast.10), custom_call_target="tpu_custom_call" | custom-call | tf_op jit(solution)/shard_map/pallas_call | solution.py:635
  23.4 0.7 %copy.11 = f32[3,16,16,128]{3,2,1,0:T(8,128)} copy(f32[3,16,16,128]{3,2,1,0:T(8,128)S(1)} %shard_map.64) | data formatting | bytes 786432

commit v6 on v5

--- a/solution.py
+++ b/solution.py
@@ -106,9 +106,6 @@
             pltpu.make_async_copy(part(src, i), part(dst, i), arrive.at[i]).start()
     later = [pltpu.make_async_copy(a, b, arrive.at[NBX + m]) for m, (a, b) in enumerate((
         (shx_in, shx), (shy_in, shy), (shz_in, shz), (frac_in, frac), (grad_in.at[1], grad.at[1])))]
-    for copy in later:
-        copy.start()
-
     barrier = pltpu.get_barrier_semaphore()
     total = jnp.int32(0)
     for way in WAYS:
@@ -506,6 +503,9 @@
     met = False
     for i in reversed(range(NBX)):
         wait_for(arrive.at[i], lambda: tiles_of(3 * BX, TY, LANES) * 3 // 2, ())
+        if i == NBX - 1:
+            for copy in later:
+                copy.start()
         bx = column(i)
         for j in range(BX):
             E0[HX + bx * BX + j, OY, :] = product(0, bx, j)
@@ -571,7 +571,7 @@
 
     forward(E1, 1, second)
 
-    def give_back(ACC, BK, k, n, meanwhile):
+    def give_back(ACC, BK, k, n):
         collect(k, EG - 1, halo=place(up))
         if NS == 2:
             collect(k, 0, halo=1 - up)
@@ -579,7 +579,6 @@
         for q in range(XG, XG + G):
             collect(k, q, ACC)
         return_rest(ACC, BK, n)
-        meanwhile()
         return_x(k, BK, n, 1)
 
     def backward(ACC, BK, n, each):
@@ -591,7 +590,8 @@
                 near_of(wait_back, n)
             each(i, column(i), received(ACC, BK, i))
 
-    give_back(ACC1, BK1, 1, 2, regular)
+    give_back(ACC1, BK1, 1, 2)
+    regular()
 
     def third(i, bx, layers):
         for j in range(BX):
@@ -604,7 +604,8 @@
         for c in range(3):
             out[c] = out[c] + STEP_SIZE * grad[1, c].astype(jnp.float32) * ADJ[...]
 
-    give_back(ACC0, BK0, 0, 3, gauss)
+    give_back(ACC0, BK0, 0, 3)
+    gauss()
 
     def fourth(i, bx, layers):
         for c in range(3):

time: 24.2 us -> 24.1 us (level)
  no operation moved by 1% of the time
where the time goes in v6:
time: 24.1 us; the launch traced here: 24 us
  Pallas kernels  23.2 us (96%)
  local copies, waits for them, and re-layouts  0.75 us (3%)
    pallas_call x1, Pallas kernels, body(): pl.pallas_call(functools.partial(kernel, shape), out_shape=jax.ShapeDtype...  23.2 us
    unnamed x1, local copies, waits for them, and re-layouts  0.75 us

profile of v6, /device:TPU:0, one launch (start us, length us, event | category | flops | bytes accessed | tf_op | source)
XLA Modules:
  0.0 24.0 jit_solution(8922754180332386989)
XLA Ops:
  0.0 23.2 %shard_map.64 = f32[3,16,16,128]{3,2,1,0:T(8,128)S(1)} custom-call(f32[3,16,16,128]{3,2,1,0:T(8,128)} %vel_in.1, bf16[2,3,16,16,128]{4,3,2,1,0:T(8,128)(2,1)} %grad_in.1, s32[2,2,1,2]{3,2,1,0:T(1,128)} %bitcast.11, s32[2,2,1,2]{3,2,1,0:T(1,128)} %bitcast.12, s32[2,2,1,2]{3,2,1,0:T(1,128)} %bitcast.13, s32[2,2,2,1,3]{4,3,2,1,0:T(1,128)} %bitcast.10), custom_call_target="tpu_custom_call" | custom-call | tf_op jit(solution)/shard_map/pallas_call | solution.py:636
  23.2 0.7 %copy.11 = f32[3,16,16,128]{3,2,1,0:T(8,128)} copy(f32[3,16,16,128]{3,2,1,0:T(8,128)S(1)} %shard_map.64) | data formatting | bytes 786432

commit v7 on v6

--- a/solution.py
+++ b/solution.py
@@ -234,17 +234,22 @@
         base = {0: 0, -1: EX, 1: EX + EG}[way[2]]
         return ref.at[slice(base + xs.start, base + xs.stop), ys, :]
 
-    def forward_x(E, k, n):
+    def forward_x(E, k, n, part):
         for h, ok in SIDES:
             mine, g, into = pl.ds(HX + h * (TX - HX), HX), XG + h * (G - XG), LX.at[k, place(1 - h)]
 
-            def send_rows(rows, where, y, ok, came):
-                to_device(E.at[mine, rows, :], into.at[0:HX, where, :], beside(h, y), ok, came)
+            def send_rows(rows, where, y, ok, came, parts=(0, 1)):
+                if 0 in parts:
+                    to_device(E.at[mine, rows, :], into.at[0:HX, where, :], beside(h, y), ok, came)
+                if 1 not in parts:
+                    return
                 for z in (-1, 1):
                     to_device(SP.at[k, (z + 1) // 2, g, rows, :], into.at[HX + (1 - z) // 2, where, :],
                               beside(h, y, z), both(ok, has((0, 0, z))), came)
 
-            send_rows(A, pl.ds(multiple(HY * (1 - even)), HY), even, ok, sem(n, 0, 1 - h))
+            send_rows(A, pl.ds(multiple(HY * (1 - even)), HY), even, ok, sem(n, 0, 1 - h), (part,))
+            if part == 0:
+                continue
             send_rows(OFF, INNER, -1, both(ok, off), sem(n, 1, 1 - h))
             send_rows(B, B, 0, ok, sem(n, 1, 1 - h))
 
@@ -509,10 +514,13 @@
         bx = column(i)
         for j in range(BX):
             E0[HX + bx * BX + j, OY, :] = product(0, bx, j)
+        meet = not met and (i == NBX - 1 and NS == 1 or i == 0)
+        if meet:
+            pl.semaphore_wait(barrier, total)
+            forward_x(E0, 0, 0, 0)
         pack_column(E0, 0, bx)
-        if not met and (i == NBX - 1 and NS == 1 or i == 0):
-            pl.semaphore_wait(barrier, total)
-            forward_x(E0, 0, 0)
+        if meet:
+            forward_x(E0, 0, 0, 1)
             met = True
     for i in range(NBX):
         forward_rest(E0, 0, 0, column(i))
@@ -558,9 +566,11 @@
             for m in range(BX):
                 rows = slice(HY + by * BY, HY + (by + 1) * BY)
                 E1[HX + bx * BX + m, rows, :] = E1[HX + bx * BX + m, rows, :] + res[m]
+        if i == NBX - 1:
+            forward_x(E1, 1, 1, 0)
         pack_column(E1, 1, bx)
         if i == NBX - 1:
-            forward_x(E1, 1, 1)
+            forward_x(E1, 1, 1, 1)
         forward_rest(E1, 1, 1, bx)
 
     forward(E0, 0, first)

time: 24.1 us -> 24.1 us (level)
  no operation moved by 1% of the time
where the time goes in v7:
time: 24.1 us; the launch traced here: 24 us
  Pallas kernels  23.2 us (96%)
  local copies, waits for them, and re-layouts  0.75 us (3%)
    pallas_call x1, Pallas kernels, body(): pl.pallas_call(functools.partial(kernel, shape), out_shape=jax.ShapeDtype...  23.2 us
    unnamed x1, local copies, waits for them, and re-layouts  0.75 us

profile of v7, /device:TPU:0, one launch (start us, length us, event | category | flops | bytes accessed | tf_op | source)
XLA Modules:
  0.0 24.0 jit_solution(16723089254454811371)
XLA Ops:
  0.0 23.2 %shard_map.64 = f32[3,16,16,128]{3,2,1,0:T(8,128)S(1)} custom-call(f32[3,16,16,128]{3,2,1,0:T(8,128)} %vel_in.1, bf16[2,3,16,16,128]{4,3,2,1,0:T(8,128)(2,1)} %grad_in.1, s32[2,2,1,2]{3,2,1,0:T(1,128)} %bitcast.11, s32[2,2,1,2]{3,2,1,0:T(1,128)} %bitcast.12, s32[2,2,1,2]{3,2,1,0:T(1,128)} %bitcast.13, s32[2,2,2,1,3]{4,3,2,1,0:T(1,128)} %bitcast.10), custom_call_target="tpu_custom_call" | custom-call | tf_op jit(solution)/shard_map/pallas_call | solution.py:646
  23.2 0.7 %copy.11 = f32[3,16,16,128]{3,2,1,0:T(8,128)} copy(f32[3,16,16,128]{3,2,1,0:T(8,128)S(1)} %shard_map.64) | data formatting | bytes 786432
